TPU v7x, 32 devices: a whole 2x2x4 slice. The times are simulated.
32 devices in a mesh: gx: 8 (over y, x, core), gy: 4 (over z).
Axes of the slice: x: 2, y: 2, z: 4, core: 2. Of those that a mesh axis runs over, the one named last changes fastest.
Arguments:
- cells: bfloat16 [1024, 256, 128], P('gx', 'gy'), may hold values from -6 to 6
- cotangent: bfloat16 [1024, 256, 128], P('gx', 'gy'), may hold values from -6 to 6
- lift_weight: bfloat16 [128, 512], replicated, may hold values from -0.5 to 0.5
- drop_weight: bfloat16 [512, 128], replicated, may hold values from -0.25 to 0.25
- xmode_weight: bfloat16 [2, 16, 128, 128], P(None, 'gx'), may hold values from -0.375 to 0.375
- ymode_weight: bfloat16 [2, 8, 128, 128], replicated, may hold values from -0.375 to 0.375
- coarse_weight: bfloat16 [128, 128], replicated, may hold values from -0.5 to 0.5
- coarse_mix: bfloat16 [16, 16], replicated, may hold values from -1.5 to 1.5
Outputs:
- cell_grad: bfloat16 [1024, 256, 128], P('gx', 'gy')
- lift_grad: float32 [128, 512], replicated
- drop_grad: float32 [512, 128], replicated
- xmode_grad: float32 [2, 16, 128, 128], P(None, 'gx')
- ymode_grad: float32 [2, 8, 128, 128], replicated
- coarse_weight_grad: float32 [128, 128], replicated
- coarse_mix_grad: float32 [16, 16], replicated
All inputs are finite; a program needn't handle non-finite values.
Results may differ from a plain program's by a relative error of at most 0.006.
Values sent between devices are 32-bit elements; how exact they have to be, the bound alone decides.
A program may use at most 128 MiB of HBM per device.

v0:
```python
import math

import jax
import jax.numpy as jnp
from jax import lax
from jax.sharding import PartitionSpec as P

MODES_X = 16
MODES_Y = 8
POOL = 16


gelu_scale = 0.7978845608028654
gelu_cubic = 0.044715
highest = lax.Precision.HIGHEST


def gelu_value(values):
    tangent = jnp.tanh(gelu_scale * (values + gelu_cubic * values * values * values))
    return 0.5 * values * (1.0 + tangent)


def gelu_slope(values):
    tangent = jnp.tanh(gelu_scale * (values + gelu_cubic * values * values * values))
    return 0.5 * (1.0 + tangent) + 0.5 * values * (1.0 - tangent * tangent) * gelu_scale * (
        1.0 + 3.0 * gelu_cubic * values * values
    )


def mode_basis(mode_count, length, offset, extent):
    frequency = jnp.arange(mode_count, dtype=jnp.int32)
    places = offset + jnp.arange(extent, dtype=jnp.int32)
    phase_index = frequency[:, None] * places[None, :] % length
    angles = phase_index.astype(jnp.float32) * (2.0 * math.pi / length)
    return jnp.concatenate([jnp.cos(angles), -jnp.sin(angles)], axis=0)


def mix_modes(spectrum, weights):

    def product(former, latter):
        return jnp.einsum("mrc,mcd->mrd", former, latter, precision=highest)

    real_out = product(spectrum[0], weights[0]) - product(spectrum[1], weights[1])
    imaginary_out = product(spectrum[0], weights[1]) + product(spectrum[1], weights[0])
    return jnp.stack([real_out, imaginary_out])


def mix_back(spectrum, gradient, weights):

    def contract_cells(former, latter):
        return jnp.einsum("mrc,mrd->mcd", former, latter, precision=highest)

    def contract_channels(former, latter):
        return jnp.einsum("mrd,mcd->mrc", former, latter, precision=highest)

    weight_real = contract_cells(spectrum[0], gradient[0]) + contract_cells(
        spectrum[1], gradient[1]
    )
    weight_imaginary = contract_cells(spectrum[0], gradient[1]) - contract_cells(
        spectrum[1], gradient[0]
    )
    spec_real = contract_channels(gradient[0], weights[0]) + contract_channels(
        gradient[1], weights[1]
    )
    spec_imaginary = contract_channels(gradient[1], weights[0]) - contract_channels(
        gradient[0], weights[1]
    )
    return (jnp.stack([weight_real, weight_imaginary]), jnp.stack([spec_real, spec_imaginary]))


def row_reduce(partial_spec):
    return lax.psum_scatter(partial_spec, "gx", scatter_dimension=1, tiled=True)


def row_return(owned_spec):
    return lax.all_gather(owned_spec, "gx", axis=1, tiled=True)


def column_reduce(partial_spec):
    return lax.psum_scatter(partial_spec, "gy", scatter_dimension=2, tiled=True)


def column_return(owned_spec):
    return lax.all_gather(owned_spec, "gy", axis=2, tiled=True)


def coarse_columns(coarse_block):
    return lax.all_gather(coarse_block, "gy", axis=1, tiled=True)


def upsample(coarse_field, row_count, column_count, channels):
    spread = jnp.broadcast_to(
        coarse_field[:, None, :, None, :],
        (row_count // POOL, POOL, column_count // POOL, POOL, channels),
    )
    return spread.reshape(row_count, column_count, channels)


def on_device(
    cells,
    cotangent,
    lift_weight,
    drop_weight,
    xmode_weight,
    ymode_weight,
    coarse_weight,
    coarse_mix,
):
    row_count, column_count, channels = cells.shape
    row_total = row_count * lax.axis_size("gx")
    column_total = column_count * lax.axis_size("gy")
    coarse_rows = row_count // POOL
    coarse_width = column_count // POOL
    row_basis = mode_basis(MODES_X, row_total, lax.axis_index("gx") * row_count, row_count)
    column_basis = mode_basis(
        MODES_Y, column_total, lax.axis_index("gy") * column_count, column_count
    )
    row_weight = xmode_weight.astype(jnp.float32)
    column_weight = ymode_weight.astype(jnp.float32)
    coarse_float = coarse_weight.astype(jnp.float32)
    mixing_float = coarse_mix.astype(jnp.float32)
    flat_cells = cells.reshape(row_count, column_count * channels)
    row_partial = jnp.dot(
        row_basis.astype(jnp.bfloat16), flat_cells, preferred_element_type=jnp.float32
    ) * (1.0 / math.sqrt(row_total))
    row_owned = row_reduce(row_partial.reshape(2, MODES_X, column_count, channels))
    row_mixed = row_return(mix_modes(row_owned, row_weight))
    row_field = jnp.dot(
        row_basis.T, row_mixed.reshape(2 * MODES_X, column_count * channels), precision=highest
    ) * (1.0 / math.sqrt(MODES_X))
    column_partial = jnp.einsum(
        "ry,xyc->rxc", column_basis.astype(jnp.bfloat16), cells, preferred_element_type=jnp.float32
    ) * (1.0 / math.sqrt(column_total))
    column_owned = column_reduce(column_partial.reshape(2, MODES_Y, row_count, channels))
    column_mixed = column_return(mix_modes(column_owned, column_weight))
    column_field = jnp.einsum(
        "ry,rxc->xyc",
        column_basis,
        column_mixed.reshape(2 * MODES_Y, row_count, channels),
        precision=highest,
    ) * (1.0 / math.sqrt(MODES_Y))
    pooled_own = cells.astype(jnp.float32).reshape(
        coarse_rows, POOL, coarse_width, POOL, channels
    ).sum(axis=(1, 3)) * (1.0 / POOL)
    pooled = coarse_columns(pooled_own)
    coarse_pre = jnp.einsum("ijc,cd->ijd", pooled, coarse_float, precision=highest)
    coarse_act = gelu_value(coarse_pre)
    column_offset = lax.axis_index("gy") * coarse_width
    mixing_rows = lax.dynamic_slice_in_dim(mixing_float, column_offset, coarse_width, 0)
    coarse_own = jnp.einsum("jk,ikc->ijc", mixing_rows, coarse_act, precision=highest)
    summed = (
        row_field.reshape(row_count, column_count, channels)
        + column_field
        + upsample(coarse_own, row_count, column_count, channels)
    )
    ffn_input = summed.reshape(row_count * column_count, channels).astype(jnp.bfloat16)
    hidden_before = jnp.dot(ffn_input, lift_weight, preferred_element_type=jnp.float32)
    hidden_after = gelu_value(hidden_before).astype(jnp.bfloat16)
    cotangent_rows = cotangent.reshape(row_count * column_count, channels)
    drop_partial = jnp.einsum(
        "nf,nc->fc", hidden_after, cotangent_rows, preferred_element_type=jnp.float32
    )
    after_grad = jnp.einsum(
        "nc,fc->nf", cotangent_rows, drop_weight, preferred_element_type=jnp.float32
    )
    before_grad = (after_grad * gelu_slope(hidden_before)).astype(jnp.bfloat16)
    lift_partial = jnp.einsum(
        "nc,nf->cf", ffn_input, before_grad, preferred_element_type=jnp.float32
    )
    summed_grad = jnp.einsum(
        "nf,cf->nc", before_grad, lift_weight, preferred_element_type=jnp.float32
    )
    summed_cells = summed_grad.reshape(row_count, column_count, channels)
    row_back_partial = jnp.dot(
        row_basis, summed_grad.reshape(row_count, column_count * channels), precision=highest
    ) * (1.0 / math.sqrt(MODES_X))
    row_back = row_reduce(row_back_partial.reshape(2, MODES_X, column_count, channels))
    row_weight_partial, row_spec_grad = mix_back(row_owned, row_back, row_weight)
    row_spec_full = row_return(row_spec_grad)
    row_cell_grad = jnp.dot(
        row_basis.T, row_spec_full.reshape(2 * MODES_X, column_count * channels), precision=highest
    ) * (1.0 / math.sqrt(row_total))
    column_back_partial = jnp.einsum(
        "ry,xyc->rxc", column_basis, summed_cells, precision=highest
    ) * (1.0 / math.sqrt(MODES_Y))
    column_back = column_reduce(column_back_partial.reshape(2, MODES_Y, row_count, channels))
    column_weight_partial, column_spec_grad = mix_back(column_owned, column_back, column_weight)
    column_spec_full = column_return(column_spec_grad)
    column_cell_grad = jnp.einsum(
        "ry,rxc->xyc",
        column_basis,
        column_spec_full.reshape(2 * MODES_Y, row_count, channels),
        precision=highest,
    ) * (1.0 / math.sqrt(column_total))
    coarse_grad_own = summed_cells.reshape(coarse_rows, POOL, coarse_width, POOL, channels).sum(
        axis=(1, 3)
    )
    coarse_grad = coarse_columns(coarse_grad_own)
    coarse_act_grad = jnp.einsum("jk,ijc->ikc", mixing_float, coarse_grad, precision=highest)
    mixing_partial = jnp.einsum("ijc,ikc->jk", coarse_grad, coarse_act, precision=highest)
    coarse_pre_grad = coarse_act_grad * gelu_slope(coarse_pre)
    coarse_weight_partial = jnp.einsum("ijc,ijd->cd", pooled, coarse_pre_grad, precision=highest)
    pre_grad_own = lax.dynamic_slice_in_dim(coarse_pre_grad, column_offset, coarse_width, 1)
    pooled_grad = jnp.einsum("ijd,cd->ijc", pre_grad_own, coarse_float, precision=highest) * (
        1.0 / POOL
    )
    cell_grad = (
        cotangent.astype(jnp.float32)
        + row_cell_grad.reshape(row_count, column_count, channels)
        + column_cell_grad
        + upsample(pooled_grad, row_count, column_count, channels)
    ).astype(jnp.bfloat16)
    xmode_grad = lax.psum(row_weight_partial, "gy")
    lift_grad, drop_grad, ymode_grad = lax.psum(
        (lift_partial, drop_partial, column_weight_partial), ("gx", "gy")
    )
    coarse_weight_grad, coarse_mix_grad = lax.psum((coarse_weight_partial, mixing_partial), "gx")
    return (
        cell_grad,
        lift_grad,
        drop_grad,
        xmode_grad,
        ymode_grad,
        coarse_weight_grad,
        coarse_mix_grad,
    )


def solution(mesh):
    in_specs = (
        P("gx", "gy", None),
        P("gx", "gy", None),
        P(),
        P(),
        P(None, "gx", None, None),
        P(),
        P(),
        P(),
    )
    out_specs = (P("gx", "gy", None), P(), P(), P(None, "gx", None, None), P(), P(), P())
    return jax.shard_map(
        on_device, mesh=mesh, in_specs=in_specs, out_specs=out_specs, check_vma=False
    )
```

profile of v0, /device:TPU:1, one launch (start us, length us, event | category | flops | bytes accessed | tf_op | source)
XLA Modules:
  0.0 477.0 jit_solution(4133987111560620458)
XLA Ops:
  8.2 3.1 fusion.17
  15.6 54.9 %all-reduce.11.cloned.1.call-done = f32[2,16,64,128]{3,2,1,0:T(8,128)} async-done(((f32[2,16,64,128]{3,2,1,0:T(8,128)}), f32[2,16,64,128]{3,2,1,0:T(8,128)}) %all-reduce.11.cloned.1.call-update) | async-done | bytes 1048592
  81.5 10.9 %all_gather.20 = f32[8,16,128]{2,0,1:T(8,128)S(1)} all-gather(f32[8,4,128]{2,0,1:T(8,128)S(1)} %copy_multiply_fusion), channel_id=1, replica_groups=mesh['gx'=8,'gy'=4] {'gy'}, dimensions={1}, use_global_device_ids=true | all-gather | bytes 81920 | tf_op jit(solution)/shard_map/all_gather | solution.py:88
  92.7 6.6 %all-gather.5.cloned.1.call-done = f32[2,16,64,128]{3,2,1,0:T(8,128)} async-done(((f32[2,2,64,128]{3,2,1,0:T(8,128)}), f32[2,16,64,128]{3,2,1,0:T(8,128)}) %all-gather.5.cloned.1.call-update) | async-done | bytes 1048592 | tf_op jit(solution)/shard_map/all_gather | solution.py:76
  99.3 4.8 %fusion.13 = f32[16,8,64,128]{3,1,2,0:T(8,128)S(1)} fusion(f32[4,8,64,128]{3,2,1,0:T(8,128)} %bitcast.239, f32[16,128]{1,0:T(8,128)S(1)} %get-tuple-element.15, f32[16,128]{1,0:T(8,128)S(1)} %get-tuple-element.14), kind=kOutput, calls=%fused_computation.23 | convolution fusion | flops 403705856 | bytes 5259264 | tf_op jit(solution)/shard_map/dot_general | solution.py:128
  104.2 2.7 copy.55
  106.8 21.8 %all-gather.7.cloned.1.call-done = f32[2,8,128,128]{3,2,1,0:T(8,128)} async-done(((f32[2,8,32,128]{3,2,1,0:T(8,128)}), f32[2,8,128,128]{3,2,1,0:T(8,128)}) %all-gather.7.cloned.1.call-update) | async-done | bytes 1048592 | tf_op jit(solution)/shard_map/all_gather | solution.py:84
  130.8 5.5 %fusion.12 = bf16[128,64,128]{2,1,0:T(8,128)(2,1)S(1)} fusion(f32[128,64,128]{2,1,0:T(8,128)S(1)} %bitcast.232, f32[16,8,64,128]{3,2,1,0:T(8,128)S(1)} %copy-done.6, f32[16,128,128]{2,1,0:T(8,128)} %bitcast.240, f32[8,64]{1,0:T(8,128)S(1)} %get-tuple-element.13, f32[8,64]{1,0:T(8,128)S(1)} %get-tuple-element.12), kind=kOutput, calls=%fused_computation.21 | convolution fusion | flops 205521920 | bytes 11538432 | tf_op jit(solution)/shard_map/ry,rxc->xyc/dot_general | solution.py:136
  138.7 11.7 %fusion.6 = bf16[8192,512]{1,0:T(8,128)(2,1)S(1)} fusion(f32[8192,512]{1,0:T(8,128)S(1)} %fusion.155, bf16[8192,128]{1,0:T(8,128)(2,1)S(1)} %bitcast.236, bf16[512,128]{1,0:T(8,128)(2,1)S(1)} %copy-done.15), kind=kOutput, calls=%fused_computation.8 | convolution fusion | flops 1153433600 | bytes 27394048 | tf_op jit(solution)/shard_map/nc,fc->nf/dot_general | solution.py:163
  150.5 3.3 copy-done.2
  153.7 4.3 fusion.156
  158.0 5.0 %reshape.90 = f32[128,8192]{1,0:T(8,128)} reshape(f32[8192,128]{1,0:T(8,128)} %fusion.156) | data formatting | bytes 8388608 | tf_op jit(solution)/shard_map/reshape | solution.py:175
  165.6 10.3 %all_gather.23 = f32[8,16,128]{2,0,1:T(8,128)S(1)} all-gather(f32[8,4,128]{2,0,1:T(8,128)S(1)} %copy.39), channel_id=1, replica_groups=mesh['gx'=8,'gy'=4] {'gy'}, dimensions={1}, use_global_device_ids=true | all-gather | bytes 81920 | tf_op jit(solution)/shard_map/all_gather | solution.py:88
  177.1 4.0 fusion.20
  182.3 3.8 fusion.21
  187.5 53.7 %all-reduce.15.cloned.1.call-done = (f32[2,16,64,128]{3,2,1,0:T(8,128)}, f32[128,128]{1,0:T(8,128)}) async-done(((f32[2,16,64,128]{3,2,1,0:T(8,128)}, f32[128,128]{1,0:T(8,128)}), (f32[2,16,64,128]{3,2,1,0:T(8,128)}, f32[128,128]{1,0:T(8,128)})) %all-reduce.15.cloned.1.call-update) | async-done | bytes 1114128
  252.8 11.0 %fusion.7 = f32[512,128]{1,0:T(8,128)} fusion(bf16[8192,128]{1,0:T(8,128)(2,1)} %bitcast.235, f32[8192,512]{1,0:T(8,128)} %copy-done.3), kind=kOutput, calls=%fused_computation.14 | convolution fusion | flops 1111490560 | bytes 19136512 | tf_op jit(solution)/shard_map/nf,nc->fc/dot_general | solution.py:160
  264.1 5.5 %fusion.157 = f32[128,512]{1,0:T(8,128)} fusion(bf16[8192,128]{1,0:T(8,128)(2,1)S(1)} %bitcast.228, bf16[8192,512]{1,0:T(8,128)(2,1)} %copy-done.2), kind=kOutput, calls=%fused_computation.215 | convolution fusion | flops 1073741824 | bytes 10747904 | tf_op jit(solution)/shard_map/nc,nf->cf/dot_general | solution.py:167
  280.8 14.0 %psum.47 = f32[16,16]{1,0:T(8,128)} all-reduce(f32[16,16]{1,0:T(8,128)S(1)} %convolution_bitcast_fusion.3), channel_id=1, replica_groups=mesh['gx'=8,'gy'=4] {'gx'}, use_global_device_ids=true, to_apply=%region_11.12 | all-reduce | flops 256 | bytes 2048 | tf_op jit(solution)/shard_map/psum | solution.py:217
  294.8 4.8 %fusion.14 = f32[16,8,64,128]{3,1,2,0:T(8,128)S(1)} fusion(f32[4,8,64,128]{3,2,1,0:T(8,128)} %bitcast.237, f32[16,128]{1,0:T(8,128)S(1)} %get-tuple-element.15, f32[16,128]{1,0:T(8,128)S(1)} %get-tuple-element.14), kind=kOutput, calls=%fused_computation.24 | convolution fusion | flops 403705856 | bytes 5259264 | tf_op jit(solution)/shard_map/dot_general | solution.py:180
  299.7 2.7 copy.58
  304.6 7.0 %fusion.10 = bf16[128,64,128]{2,1,0:T(8,128)(2,1)} fusion(f32[128,64,128]{2,1,0:T(8,128)S(1)} %bitcast.231, f32[16,8,64,128]{3,2,1,0:T(8,128)S(1)} %copy-done.5, bf16[128,64,128]{2,1,0:T(8,128)(2,1)S(1)} %copy-done.12, f32[16,128,128]{2,1,0:T(8,128)} %bitcast.238, f32[8,64]{1,0:T(8,128)S(1)} %get-tuple-element.13, f32[8,64]{1,0:T(8,128)S(1)} %get-tuple-element.12), kind=kOutput, calls=%fused_computation.18 | convolution fusion | flops 207619072 | bytes 13635584 | tf_op jit(solution)/shard_map/ry,rxc->xyc/dot_general | solution.py:189
  311.6 9.4 %all-reduce.9.cloned.1.call-done = f32[2,2,128,128]{3,2,1,0:T(8,128)} async-done(((f32[2,2,128,128]{3,2,1,0:T(8,128)}), f32[2,2,128,128]{3,2,1,0:T(8,128)}) %all-reduce.9.cloned.1.call-update) | async-done | bytes 262160 | tf_op jit(solution)/shard_map/psum | solution.py:213
  321.0 140.3 %all-reduce.13.cloned.1.call-done = (f32[128,512]{1,0:T(8,128)}, f32[512,128]{1,0:T(8,128)}, f32[2,8,128,128]{3,2,1,0:T(8,128)}) async-done(((f32[128,512]{1,0:T(8,128)}, f32[512,128]{1,0:T(8,128)}, f32[2,8,128,128]{3,2,1,0:T(8,128)}), (f32[128,512]{1,0:T(8,128)}, f32[512,128]{1,0:T(8,128)}, f32[2,8,128,128]{3,2,1,0:T(8,128)})) %all-reduce.13.cloned.1.call-update) | async-done | bytes 1572880 | tf_op jit(solution)/shard_map/psum | solution.py:214
  (119 shorter events, 58.8 us)
Async XLA Ops:
  8.0 128.3 %copy-start = (bf16[128,512]{1,0:T(8,128)(2,1)S(1)}, bf16[128,512]{1,0:T(8,128)(2,1)}, u32[]{:S(2)}) copy-start(bf16[128,512]{1,0:T(8,128)(2,1)} %param.10) | copy-start | bytes 393220
  8.0 4.6 copy-start.4
  8.0 62.5 %all-reduce.11.cloned.1.call-start = ((), (), s32[]{:S(2)}) async-start(), calls=%async_computation.9 | async-start | bytes 2097152
  12.4 58.1 %copy-start.10 = (bf16[2,2,128,128]{3,2,1,0:T(8,128)(2,1)S(1)}, bf16[2,2,128,128]{3,2,1,0:T(8,128)(2,1)}, u32[]{:S(2)}) copy-start(bf16[2,2,128,128]{3,2,1,0:T(8,128)(2,1)} %param.12) | copy-start | bytes 393220
  12.4 63.0 %copy-start.7 = (bf16[2,8,128,128]{3,2,1,0:T(8,128)(2,1)S(1)}, bf16[2,8,128,128]{3,2,1,0:T(8,128)(2,1)}, u32[]{:S(2)}) copy-start(bf16[2,8,128,128]{3,2,1,0:T(8,128)(2,1)} %param.13) | copy-start | bytes 1572868
  12.4 62.9 %reduce-scatter.9.cloned.1.call-start = ((), (), s32[]{:S(2)}) async-start(), calls=%async_computation.3 | async-start | bytes 1310720 | tf_op jit(solution)/shard_map/reduce_scatter | solution.py:80
  14.3 78.1 %copy-start.13 = (bf16[128,128]{1,0:T(8,128)(2,1)S(1)}, bf16[128,128]{1,0:T(8,128)(2,1)}, u32[]{:S(2)}) copy-start(bf16[128,128]{1,0:T(8,128)(2,1)} %param.14) | copy-start | bytes 98308
  14.3 78.3 %copy-start.16 = (bf16[16,16]{1,0:T(8,128)(2,1)S(1)}, bf16[16,16]{1,0:T(8,128)(2,1)}, u32[]{:S(2)}) copy-start(bf16[16,16]{1,0:T(8,128)(2,1)} %param.15) | copy-start | bytes 1540
  14.3 85.0 %all-gather.5.cloned.1.call-start = ((), (), s32[]{:S(2)}) async-start(), calls=%async_computation.2 | async-start | bytes 1179648 | tf_op jit(solution)/shard_map/all_gather | solution.py:76
  75.3 53.3 %all-gather.7.cloned.1.call-start = ((), (), s32[]{:S(2)}) async-start(), calls=%async_computation.4 | async-start | bytes 1310720 | tf_op jit(solution)/shard_map/all_gather | solution.py:84
  81.0 160.2 %all-reduce.15.cloned.1.call-start = ((), (), s32[]{:S(2)}) async-start(), calls=%async_computation.11 | async-start | bytes 2228224
  136.3 2.4 copy-start.11
  138.7 11.8 %copy-start.3 = (f32[8192,512]{1,0:T(8,128)}, f32[8192,512]{1,0:T(8,128)S(1)}, u32[]{:S(2)}) copy-start(f32[8192,512]{1,0:T(8,128)S(1)} %fusion.155) | copy-start | bytes 50331652
  150.4 3.3 copy-start.2
  182.2 64.1 %reduce-scatter.11.cloned.1.call-start = ((), (), s32[]{:S(2)}) async-start(), calls=%async_computation.6 | async-start | bytes 1310720 | tf_op jit(solution)/shard_map/reduce_scatter | solution.py:80
  187.4 107.4 %all-gather.9.cloned.1.call-start = ((), (), s32[]{:S(2)}) async-start(), calls=%async_computation.5 | async-start | bytes 1179648 | tf_op jit(solution)/shard_map/all_gather | solution.py:76
  246.2 56.1 %all-gather.11.cloned.1.call-start = ((), (), s32[]{:S(2)}) async-start(), calls=%async_computation.7 | async-start | bytes 1310720 | tf_op jit(solution)/shard_map/all_gather | solution.py:84
  252.8 68.2 %all-reduce.9.cloned.1.call-start = ((), (), s32[]{:S(2)}) async-start(), calls=%async_computation.8 | async-start | bytes 524288 | tf_op jit(solution)/shard_map/psum | solution.py:213
  264.0 11.4 %copy-start.8 = (f32[2,8,32,128]{3,2,1,0:T(8,128)S(1)}, f32[2,8,32,128]{3,2,1,0:T(8,128)}, u32[]{:S(2)}) copy-start(f32[2,8,32,128]{3,2,1,0:T(8,128)} %reduce-scatter.9.cloned.1.call-done) | copy-start | bytes 786436
  264.0 11.4 %copy-start.9 = (f32[2,8,32,128]{3,2,1,0:T(8,128)S(1)}, f32[2,8,32,128]{3,2,1,0:T(8,128)}, u32[]{:S(2)}) copy-start(f32[2,8,32,128]{3,2,1,0:T(8,128)} %reduce-scatter.11.cloned.1.call-done) | copy-start | bytes 786436
  275.4 185.9 %all-reduce.13.cloned.1.call-start = ((), (), s32[]{:S(2)}) async-start(), calls=%async_computation.10 | async-start | bytes 3145728 | tf_op jit(solution)/shard_map/psum | solution.py:214
  299.7 3.2 copy-start.12
  304.6 164.0 %copy-start.14 = (f32[128,128]{1,0:T(8,128)S(1)}, f32[128,128]{1,0:T(8,128)}, u32[]{:S(2)}) copy-start(f32[128,128]{1,0:T(8,128)} %get-tuple-element.21) | copy-start | bytes 196612
  304.6 164.6 %copy-start.1 = (bf16[128,512]{1,0:T(8,128)(2,1)S(1)}, bf16[128,512]{1,0:T(8,128)(2,1)}, u32[]{:S(2)}) copy-start(bf16[128,512]{1,0:T(8,128)(2,1)} %param.10) | copy-start | bytes 393220
  (4 other events, 8.7 us)
Sparse Core Ops, SparseCore 0:
  12.6 57.8 all-reduce.10
  75.4 23.8 all-gather.4
  101.5 27.0 all-gather.6
  182.4 58.8 all-reduce.14
  246.4 23.9 all-gather.8
  272.3 29.9 all-gather.10
Sparse Core Ops, SparseCore 1:
  15.8 28.5 reduce-scatter.8
  187.5 29.1 reduce-scatter.10
  275.4 45.5 all-reduce.8
  327.3 133.9 all-reduce.12
where the time goes:
time: 484 us; the launch traced here: 477 us
  waiting for transfers between devices  287 us (59%)
  matrix products  98.1 us (20%)
  blocking collectives  35.2 us (7%)
  local copies, waits for them, and re-layouts  31.6 us (7%)
  between operations  17.2 us (4%)
  other arithmetic  7.65 us (2%)
    psum x1, waiting for transfers between devices, on_device(): lax.psum((lift_partial, drop_partial, column_weight_partial), ('gx', 'gy'))  140 us
    unnamed x12, waiting for transfers between devices  109 us
    unnamed x46, local copies, waits for them, and re-layouts  23 us
    all_gather x2, waiting for transfers between devices, column_return(): return lax.all_gather(owned_spec, 'gy', axis=2, tiled=True)  21.8 us
    all_gather x2, blocking collectives, coarse_columns(): return lax.all_gather(coarse_block, 'gy', axis=1, tiled=True)  21.2 us
    psum x1, blocking collectives, on_device(): lax.psum((coarse_weight_partial, mixing_partial), 'gx')  14 us
    dot_general x1, matrix products, on_device(): jnp.einsum('nc,fc->nf', cotangent_rows, drop_weight, preferred_element_ty...  11.7 us
    dot_general x1, matrix products, on_device(): jnp.einsum('nf,nc->fc', hidden_after, cotangent_rows, preferred_element_t...  11 us
  transfers between devices with their start and end apart: 10, of which 6 were waited for; matrix products, arithmetic and copies ran while one was open for 17% of the time, Pallas kernels for 0%

commit v1 on v0

v1 whole, which is shorter than its diff:
```python
import functools
import math

import jax
import jax.numpy as jnp
import numpy as np
from jax import lax
from jax.experimental import pallas as pl
from jax.experimental.pallas import tpu as pltpu
from jax.sharding import PartitionSpec as P

MODES_X = 16
MODES_Y = 8
POOL = 16
TILE = 8

gelu_scale = 0.7978845608028654
gelu_cubic = 0.044715
MESH = pl.DeviceIdType.MESH
VMEM_SPEC = pl.BlockSpec(memory_space=pltpu.VMEM)
low = jnp.bfloat16
wide = jnp.float32


def gelu_pair(values):
    square = values * values
    tangent = jnp.tanh(values * (gelu_scale + (gelu_scale * gelu_cubic) * square))
    half = 0.5 + 0.5 * tangent
    bend = values * (0.5 * gelu_scale + (1.5 * gelu_scale * gelu_cubic) * square)
    return values * half, half + bend * (1.0 - tangent * tangent)


def dot(former, latter):
    return jnp.dot(former, latter, preferred_element_type=wide)


def dot_nt(former, latter):
    return lax.dot_general(former, latter, (((1,), (1,)), ((), ())), preferred_element_type=wide)


def dot_tn(former, latter):
    return lax.dot_general(former, latter, (((0,), (0,)), ((), ())), preferred_element_type=wide)


def basis_table(mode_count, length):
    phase = np.outer(np.arange(mode_count), np.arange(length)) % length
    angles = phase * (2.0 * math.pi / length)
    return np.concatenate([np.cos(angles), -np.sin(angles)], axis=0).astype(np.float32)


def analyse(block, first, step, xback_ref, yback_ref, row_ref, column_ref, pool_ref):
    rows, columns, channels = block.shape
    for tile in range(columns // TILE):
        own = pl.ds(tile * TILE, TILE)
        piece = block[:, tile * TILE : (tile + 1) * TILE, :].reshape(rows * TILE, channels)
        part = dot(xback_ref[...], piece.astype(low)).reshape(2 * MODES_X, TILE, channels)

        @pl.when(first)
        def _():
            row_ref[:, own, :] = part

        @pl.when(jnp.logical_not(first))
        def _():
            row_ref[:, own, :] += part

    for tile in range(rows // TILE):
        piece = block[tile * TILE : (tile + 1) * TILE].reshape(TILE * columns, channels)
        part = dot(yback_ref[...], piece.astype(low))
        column_ref[:, tile * TILE : (tile + 1) * TILE, :] = part.reshape(
            2 * MODES_Y, TILE, channels
        )
    pooled = block.sum(axis=0).reshape(columns // POOL, POOL, channels).sum(axis=1)
    pool_ref[:, pl.ds(step, 1), :] = pooled[:, None, :]


def analysis_kernel(cells_ref, xback_ref, yback_ref, row_ref, column_ref, pool_ref):
    step = pl.program_id(0)
    block = cells_ref[...].astype(wide)
    analyse(block, step == 0, step, xback_ref, yback_ref, row_ref, column_ref, pool_ref)


def synthesise(rows, columns, channels, xfore, yfore_ref, row_low, column_of, coarse_of):
    parts = []
    for tile in range(rows // TILE):
        modes = column_of(tile).reshape(2 * MODES_Y * TILE, channels).astype(low)
        parts.append(dot(yfore_ref[...], modes).reshape(TILE, columns, channels))
    field = jnp.concatenate(parts, axis=0)
    pieces = []
    for tile in range(columns // TILE):
        part = dot(xfore, row_low(tile)).reshape(rows, TILE, channels)
        pieces.append(part + coarse_of(tile * TILE // POOL))
    return field + jnp.concatenate(pieces, axis=1)


def ffn_kernel(
    cotangent_ref,
    rowf_ref,
    colf_ref,
    coarse_ref,
    lift_ref,
    liftt_ref,
    dropt_ref,
    xfore_ref,
    xback_ref,
    yfore_ref,
    yback_ref,
    row_ref,
    column_ref,
    pool_ref,
    total_ref,
    rowlow_ref,
):
    step = pl.program_id(0)
    rows, columns, channels = cotangent_ref.shape
    hidden = lift_ref.shape[1]

    @pl.when(step == 0)
    def _():
        for tile in range(columns // TILE):
            rowlow_ref[tile] = (
                rowf_ref[:, tile * TILE : (tile + 1) * TILE, :]
                .reshape(2 * MODES_X * TILE, channels)
                .astype(low)
            )
        total_ref[...] = jnp.zeros_like(total_ref)

    coarse = coarse_ref[:, pl.ds(step, 1), :]
    summed = synthesise(
        rows,
        columns,
        channels,
        xfore_ref[...],
        yfore_ref,
        lambda tile: rowlow_ref[tile],
        lambda tile: colf_ref[:, tile * TILE : (tile + 1) * TILE, :],
        lambda place: coarse[place : place + 1],
    )
    count = rows * columns
    entering = summed.reshape(count, channels).astype(low)
    cotangent = cotangent_ref[...].reshape(count, channels)
    before = dot(entering, lift_ref[...])
    value, slope = gelu_pair(before)
    after_grad = dot(cotangent, dropt_ref[...])
    before_grad = (after_grad * slope).astype(low)
    total_ref[:, 0:hidden] += dot_tn(entering, before_grad)
    total_ref[:, hidden : 2 * hidden] += dot_tn(cotangent, value.astype(low))
    back = dot(before_grad, liftt_ref[...]).reshape(rows, columns, channels)
    analyse(back, step == 0, step, xback_ref, yback_ref, row_ref, column_ref, pool_ref)


def greet(sizes):
    barrier = pltpu.get_barrier_semaphore()
    count = 0
    for axis, size in sizes:
        me = lax.axis_index(axis)
        for k in range(1, size):
            pl.semaphore_signal(
                barrier, inc=1, device_id={axis: lax.rem(me + k, size)}, device_id_type=MESH
            )
            count += 1
    pl.semaphore_wait(barrier, count)


def send(axis, size, source_of, target_of, sems):
    me = lax.axis_index(axis)
    copies = []
    for k in range(1, size):
        dest = lax.rem(me + k, size)
        copy = pltpu.make_async_remote_copy(
            src_ref=source_of(dest),
            dst_ref=target_of(k - 1),
            send_sem=sems.at[0, k - 1],
            recv_sem=sems.at[1, k - 1],
            device_id={axis: dest},
            device_id_type=MESH,
        )
        copy.start()
        copies.append(copy)
    return copies


def arrive(copies):
    for copy in copies:
        copy.wait_recv()


def leave(copies):
    for copy in copies:
        copy.wait_send()


def sum_slots(own, slots_ref):
    for k in range(slots_ref.shape[0]):
        own = own + slots_ref[k]
    return own


def share(index, extent):
    return pl.ds(pl.multiple_of(index * extent, extent), extent)


def forward_kernel(
    n,
    m,
    scales,
    rowp_ref,
    colp_ref,
    poolp_ref,
    xweight_ref,
    yweight_ref,
    cweight_ref,
    mixrows_ref,
    rowown_ref,
    colown_ref,
    rowf_ref,
    colf_ref,
    pooled_ref,
    coarse_ref,
    rowslots,
    colslots,
    sem_row,
    sem_col,
    sem_pool,
    sem_rowf,
    sem_colf,
):
    scale_rows, scale_columns = scales
    px, py = lax.axis_index("gx"), lax.axis_index("gy")
    modes = MODES_X // n
    columns, channels = rowp_ref.shape[2:]
    rows = colp_ref.shape[2] // m
    width = poolp_ref.shape[0]
    greet((("gx", n), ("gy", m)))
    to_col = send(
        "gy", m, lambda d: colp_ref.at[:, :, share(d, rows)], lambda k: colslots.at[k], sem_col
    )
    to_row = send(
        "gx", n, lambda d: rowp_ref.at[:, share(d, modes)], lambda k: rowslots.at[k], sem_row
    )
    to_pool = send(
        "gy", m, lambda d: poolp_ref, lambda k: pooled_ref.at[share(py, width)], sem_pool
    )
    pooled_ref[share(py, width)] = poolp_ref[...]

    arrive(to_row)
    spec = sum_slots(rowp_ref[:, share(px, modes)], rowslots) * scale_rows
    rowown_ref[...] = spec
    for mode in range(modes):
        both = spec[:, mode].reshape(2 * columns, channels).astype(low)
        one = dot(both, xweight_ref[0, mode])
        two = dot(both, xweight_ref[1, mode])
        gain = 1.0 / math.sqrt(MODES_X)
        rowf_ref[0, px * modes + mode] = (one[:columns] - two[columns:]) * gain
        rowf_ref[1, px * modes + mode] = (two[:columns] + one[columns:]) * gain
    to_rowf = send(
        "gx",
        n,
        lambda d: rowf_ref.at[:, share(px, modes)],
        lambda k: rowf_ref.at[:, share(px, modes)],
        sem_rowf,
    )

    arrive(to_col)
    for mode in range(MODES_Y):
        spec = colp_ref[:, mode, share(py, rows)]
        for k in range(m - 1):
            spec = spec + colslots[k, :, mode]
        spec = spec * scale_columns
        colown_ref[:, mode] = spec
        both = spec.reshape(2 * rows, channels).astype(low)
        one = dot(both, yweight_ref[0, mode])
        two = dot(both, yweight_ref[1, mode])
        gain = 1.0 / math.sqrt(MODES_Y)
        colf_ref[0, mode, share(py, rows)] = (one[:rows] - two[rows:]) * gain
        colf_ref[1, mode, share(py, rows)] = (two[:rows] + one[rows:]) * gain
    to_colf = send(
        "gy",
        m,
        lambda d: colf_ref.at[:, :, share(py, rows)],
        lambda k: colf_ref.at[:, :, share(py, rows)],
        sem_colf,
    )

    arrive(to_pool)
    total_width, coarse_rows = pooled_ref.shape[:2]
    pooled = pooled_ref[...].reshape(total_width * coarse_rows, channels) * (1.0 / POOL)
    pre = dot(pooled.astype(low), cweight_ref[...])
    act, _ = gelu_pair(pre)
    coarse_ref[...] = dot(mixrows_ref[...], act.astype(low)).reshape(coarse_ref.shape)

    arrive(to_rowf)
    arrive(to_colf)
    for copies in (to_row, to_col, to_pool, to_rowf, to_colf):
        leave(copies)


def backward_kernel(
    n,
    m,
    scales,
    cotangent_ref,
    rowp_ref,
    colp_ref,
    poolp_ref,
    total_ref,
    rowown_ref,
    colown_ref,
    pooled_ref,
    xweight_ref,
    yweight_ref,
    cweight_ref,
    mixback_ref,
    xfore_ref,
    yfore_ref,
    cell_ref,
    totalf_ref,
    xgrad_ref,
    ygrad_ref,
    cgrad_ref,
    rowslots,
    colslots,
    rowf_ref,
    colf_ref,
    grads_ref,
    pregrad_ref,
    poolgrad_ref,
    totalslots,
    totalall,
    xpart,
    xslots,
    ypart,
    yslots,
    ychunk,
    ycslots,
    cpart,
    cslots,
    rowlow_ref,
    sem_row,
    sem_col,
    sem_pool,
    sem_rowf,
    sem_colf,
    sem_t,
    sem_tg,
    sem_tf,
    sem_x,
    sem_xf,
    sem_y,
    sem_yc,
    sem_ycf,
    sem_yf,
    sem_c,
    sem_cf,
):
    scale_rows, scale_columns = scales
    px, py = lax.axis_index("gx"), lax.axis_index("gy")
    modes = MODES_X // n
    columns, channels = rowp_ref.shape[2:]
    rows = colp_ref.shape[2] // m
    width, coarse_rows = poolp_ref.shape[:2]
    greet((("gx", n), ("gy", m)))
    to_pool = send(
        "gy", m, lambda d: poolp_ref, lambda k: grads_ref.at[share(py, width)], sem_pool
    )
    to_col = send(
        "gy", m, lambda d: colp_ref.at[:, :, share(d, rows)], lambda k: colslots.at[k], sem_col
    )
    to_row = send(
        "gx", n, lambda d: rowp_ref.at[:, share(d, modes)], lambda k: rowslots.at[k], sem_row
    )
    trows = total_ref.shape[0] // n
    to_t = send(
        "gx", n, lambda d: total_ref.at[share(d, trows)], lambda k: totalslots.at[k], sem_t
    )
    grads_ref[share(py, width)] = poolp_ref[...]

    arrive(to_pool)
    total_width = grads_ref.shape[0]
    count = total_width * coarse_rows
    pooled = (pooled_ref[...].reshape(count, channels) * (1.0 / POOL)).astype(low)
    pre = dot(pooled, cweight_ref[...])
    act, slope = gelu_pair(pre)
    grads = grads_ref[...].reshape(count, channels).astype(low)
    pre_grad = dot(mixback_ref[...], grads) * slope
    pregrad_ref[...] = pre_grad.reshape(pregrad_ref.shape)
    cpart[:, 0:channels] = dot_tn(pooled, pre_grad.astype(low))
    cross = dot_nt(grads, act.astype(low))
    left = lax.broadcasted_iota(jnp.int32, (count, count), 0) % coarse_rows
    right = lax.broadcasted_iota(jnp.int32, (count, count), 1) % coarse_rows
    cross = jnp.where(left == right, cross, 0.0)
    pick = (
        lax.broadcasted_iota(jnp.int32, (channels, count), 0)
        == lax.broadcasted_iota(jnp.int32, (channels, count), 1) // coarse_rows
    ).astype(wide)
    highest = lax.Precision.HIGHEST
    half = jnp.dot(pick, cross, precision=highest, preferred_element_type=wide)
    cpart[:, channels : 2 * channels] = lax.dot_general(
        half, pick, (((1,), (1,)), ((), ())), precision=highest, preferred_element_type=wide
    )
    crows = cpart.shape[0] // n
    to_c = send("gx", n, lambda d: cpart.at[share(d, crows)], lambda k: cslots.at[k], sem_c)
    own_grad = pregrad_ref[share(py, width)].reshape(width * coarse_rows, channels)
    poolgrad_ref[...] = (dot_nt(own_grad.astype(low), cweight_ref[...]) * (1.0 / POOL)).reshape(
        poolgrad_ref.shape
    )

    def mix_back(spec, grad, real_weight, imaginary_weight):
        half_rows = spec.shape[0] // 2
        grad_low = grad.astype(low)
        turned = jnp.concatenate([grad[half_rows:], -grad[:half_rows]], axis=0).astype(low)
        spec_low = spec.astype(low)
        back = dot_nt(grad_low, real_weight) + dot_nt(turned, imaginary_weight)
        return dot_tn(spec_low, grad_low), dot_tn(spec_low, turned), back

    arrive(to_row)
    grad = sum_slots(rowp_ref[:, share(px, modes)], rowslots) * (1.0 / math.sqrt(MODES_X))
    for mode in range(modes):
        real, imaginary, back = mix_back(
            rowown_ref[:, mode].reshape(2 * columns, channels),
            grad[:, mode].reshape(2 * columns, channels),
            xweight_ref[0, mode],
            xweight_ref[1, mode],
        )
        xpart[pl.ds(mode * channels, channels)] = real
        xpart[pl.ds((modes + mode) * channels, channels)] = imaginary
        rowf_ref[0, px * modes + mode] = back[:columns] * scale_rows
        rowf_ref[1, px * modes + mode] = back[columns:] * scale_rows
    to_rowf = send(
        "gx",
        n,
        lambda d: rowf_ref.at[:, share(px, modes)],
        lambda k: rowf_ref.at[:, share(px, modes)],
        sem_rowf,
    )

    arrive(to_col)
    for mode in range(MODES_Y):
        grad = colp_ref[:, mode, share(py, rows)]
        for k in range(m - 1):
            grad = grad + colslots[k, :, mode]
        grad = grad * (1.0 / math.sqrt(MODES_Y))
        real, imaginary, back = mix_back(
            colown_ref[:, mode].reshape(2 * rows, channels),
            grad.reshape(2 * rows, channels),
            yweight_ref[0, mode],
            yweight_ref[1, mode],
        )
        ypart[pl.ds(mode * channels, channels)] = real
        ypart[pl.ds((MODES_Y + mode) * channels, channels)] = imaginary
        colf_ref[0, mode, share(py, rows)] = back[:rows] * scale_columns
        colf_ref[1, mode, share(py, rows)] = back[rows:] * scale_columns
    to_colf = send(
        "gy",
        m,
        lambda d: colf_ref.at[:, :, share(py, rows)],
        lambda k: colf_ref.at[:, :, share(py, rows)],
        sem_colf,
    )
    yrows = ypart.shape[0] // n
    to_y = send("gx", n, lambda d: ypart.at[share(d, yrows)], lambda k: yslots.at[k], sem_y)
    xrows = xpart.shape[0] // m
    to_x = send("gy", m, lambda d: xpart.at[share(d, xrows)], lambda k: xslots.at[k], sem_x)

    arrive(to_t)
    totalall[py] = sum_slots(total_ref[share(px, trows)], totalslots)
    to_tg = send("gy", m, lambda d: totalall.at[py], lambda k: totalall.at[py], sem_tg)
    arrive(to_c)
    cgrad_ref[share(px, crows)] = sum_slots(cpart[share(px, crows)], cslots)
    to_cf = send(
        "gx",
        n,
        lambda d: cgrad_ref.at[share(px, crows)],
        lambda k: cgrad_ref.at[share(px, crows)],
        sem_cf,
    )

    block = POOL

    def field(step):
        xfore = xfore_ref[pl.ds(pl.multiple_of(step * (block * TILE), block * TILE), block * TILE)]
        coarse = poolgrad_ref[:, pl.ds(step, 1), :]

        def column_of(tile):
            begin = pl.multiple_of(step * block + tile * TILE, TILE)
            return colf_ref[:, :, pl.ds(begin, TILE), :]

        got = synthesise(
            block,
            columns,
            channels,
            xfore,
            yfore_ref,
            lambda tile: rowlow_ref[tile],
            column_of,
            lambda place: coarse[place : place + 1],
        )
        own = pl.ds(pl.multiple_of(step * block, block), block)
        cell_ref[own] = (cotangent_ref[own].astype(wide) + got).astype(low)

    arrive(to_rowf)
    for tile in range(columns // TILE):
        rowlow_ref[tile] = (
            rowf_ref[:, :, tile * TILE : (tile + 1) * TILE, :]
            .reshape(2 * MODES_X * TILE, channels)
            .astype(low)
        )
    arrive(to_y)
    ychunk[...] = sum_slots(ypart[share(px, yrows)], yslots)
    ycrows = yrows // m
    to_yc = send("gy", m, lambda d: ychunk.at[share(d, ycrows)], lambda k: ycslots.at[k], sem_yc)
    arrive(to_x)
    xgrad_ref[share(py, xrows)] = sum_slots(xpart[share(py, xrows)], xslots)
    to_xf = send(
        "gy",
        m,
        lambda d: xgrad_ref.at[share(py, xrows)],
        lambda k: xgrad_ref.at[share(py, xrows)],
        sem_xf,
    )
    arrive(to_tg)
    whole_total = totalall[0]
    for k in range(1, m):
        whole_total = whole_total + totalall[k]
    totalf_ref[share(px, trows)] = whole_total
    to_tf = send(
        "gx",
        n,
        lambda d: totalf_ref.at[share(px, trows)],
        lambda k: totalf_ref.at[share(px, trows)],
        sem_tf,
    )
    arrive(to_colf)
    steps = cell_ref.shape[0] // block
    early = steps // 2

    @pl.loop(0, early)
    def _(step):
        field(step)

    arrive(to_yc)
    own_y = pl.ds(pl.multiple_of(px * yrows + py * ycrows, ycrows), ycrows)
    ygrad_ref[own_y] = sum_slots(ychunk[share(py, ycrows)], ycslots)
    to_ycf = send("gy", m, lambda d: ygrad_ref.at[own_y], lambda k: ygrad_ref.at[own_y], sem_ycf)
    arrive(to_ycf)
    to_yf = send(
        "gx",
        n,
        lambda d: ygrad_ref.at[share(px, yrows)],
        lambda k: ygrad_ref.at[share(px, yrows)],
        sem_yf,
    )

    @pl.loop(early, steps)
    def _(step):
        field(step)

    for copies in (to_cf, to_xf, to_tf, to_yf):
        arrive(copies)
    for copies in (
        to_pool,
        to_col,
        to_row,
        to_t,
        to_c,
        to_rowf,
        to_colf,
        to_y,
        to_x,
        to_tg,
        to_cf,
        to_yc,
        to_xf,
        to_tf,
        to_ycf,
        to_yf,
    ):
        leave(copies)


def spread(rows, columns, row_of, column_of, table, keep):
    left = (
        row_of(lax.broadcasted_iota(jnp.int32, (rows, table.shape[0]), 0))
        == lax.broadcasted_iota(jnp.int32, (rows, table.shape[0]), 1)
    ).astype(low)
    right = (
        column_of(lax.broadcasted_iota(jnp.int32, (table.shape[1], columns), 1))
        == lax.broadcasted_iota(jnp.int32, (table.shape[1], columns), 0)
    ).astype(low)
    full = dot(dot(left, table).astype(low), right)
    place_row = lax.broadcasted_iota(jnp.int32, (rows, columns), 0)
    place_column = lax.broadcasted_iota(jnp.int32, (rows, columns), 1)
    return jnp.where(keep(place_row, place_column), full, 0.0).astype(low)


def remote(size):
    return pltpu.SemaphoreType.DMA((2, size - 1))


def on_device(
    n,
    m,
    cells,
    cotangent,
    lift_weight,
    drop_weight,
    xmode_weight,
    ymode_weight,
    coarse_weight,
    coarse_mix,
):
    rows, columns, channels = cells.shape
    hidden = lift_weight.shape[1]
    row_total, column_total = rows * n, columns * m
    coarse_rows, width = rows // POOL, columns // POOL
    total_width = width * m
    modes = MODES_X // n
    row_share = rows // m
    px, py = lax.axis_index("gx"), lax.axis_index("gy")
    row_basis = lax.dynamic_slice_in_dim(
        jnp.asarray(basis_table(MODES_X, row_total)), px * rows, rows, 1
    ).astype(low)
    column_basis = lax.dynamic_slice_in_dim(
        jnp.asarray(basis_table(MODES_Y, column_total)), py * columns, columns, 1
    ).astype(low)
    by_tile = lambda v: v // TILE
    same_tile = lambda r, c: r % TILE == c % TILE
    xfore = spread(rows * TILE, 2 * MODES_X * TILE, by_tile, by_tile, row_basis.T, same_tile)
    xback = spread(2 * MODES_X * TILE, rows * TILE, by_tile, by_tile, row_basis, same_tile)
    in_columns = lambda v: v % columns
    yfore = spread(
        TILE * columns,
        2 * MODES_Y * TILE,
        in_columns,
        by_tile,
        column_basis.T,
        lambda r, c: r // columns == c % TILE,
    )
    yback = spread(
        2 * MODES_Y * TILE,
        TILE * columns,
        by_tile,
        in_columns,
        column_basis,
        lambda r, c: r % TILE == c // columns,
    )
    by_coarse = lambda v: v // coarse_rows
    same_coarse = lambda r, c: r % coarse_rows == c % coarse_rows
    mix_rows = lax.dynamic_slice_in_dim(coarse_mix, py * width, width, 0)
    mix_fore = spread(
        width * coarse_rows, total_width * coarse_rows, by_coarse, by_coarse, mix_rows, same_coarse
    )
    mix_back = spread(
        total_width * coarse_rows,
        total_width * coarse_rows,
        by_coarse,
        by_coarse,
        coarse_mix.T,
        same_coarse,
    )
    steps = rows // POOL
    block_spec = pl.BlockSpec((POOL, columns, channels), lambda i: (i, 0, 0))

    def whole(*shape):
        return pl.BlockSpec(shape, lambda i: (0,) * len(shape))

    xback_spec = pl.BlockSpec((2 * MODES_X * TILE, POOL * TILE), lambda i: (0, i))
    xfore_spec = pl.BlockSpec((POOL * TILE, 2 * MODES_X * TILE), lambda i: (i, 0))
    column_spec = pl.BlockSpec((2 * MODES_Y, POOL, channels), lambda i: (0, i, 0))
    analysis_out = [
        jax.ShapeDtypeStruct((2 * MODES_X, columns, channels), wide),
        jax.ShapeDtypeStruct((2 * MODES_Y, rows, channels), wide),
        jax.ShapeDtypeStruct((width, coarse_rows, channels), wide),
    ]
    analysis_specs = [
        whole(2 * MODES_X, columns, channels),
        column_spec,
        whole(width, coarse_rows, channels),
    ]
    sequential = pltpu.CompilerParams(dimension_semantics=("arbitrary",))
    row_part, column_part, pool_part = pl.pallas_call(
        analysis_kernel,
        grid=(steps,),
        in_specs=[block_spec, xback_spec, whole(*yback.shape)],
        out_specs=analysis_specs,
        out_shape=analysis_out,
        compiler_params=sequential,
        name="analysis",
    )(cells, xback, yback)

    scales = (1.0 / math.sqrt(row_total), 1.0 / math.sqrt(column_total))
    row_shape = (2, MODES_X, columns, channels)
    column_shape = (2, MODES_Y, rows, channels)
    f32 = lambda *shape: jax.ShapeDtypeStruct(shape, wide)
    vm = lambda *shape: pltpu.VMEM(shape, wide)
    row_own, column_own, row_full, column_full, pooled, coarse_own = pl.pallas_call(
        functools.partial(forward_kernel, n, m, scales),
        out_shape=[
            f32(2, modes, columns, channels),
            f32(2, MODES_Y, row_share, channels),
            f32(*row_shape),
            f32(*column_shape),
            f32(total_width, coarse_rows, channels),
            f32(width, coarse_rows, channels),
        ],
        in_specs=[VMEM_SPEC] * 7,
        out_specs=[VMEM_SPEC] * 6,
        scratch_shapes=[
            vm(n - 1, 2, modes, columns, channels),
            vm(m - 1, 2, MODES_Y, row_share, channels),
            remote(n),
            remote(m),
            remote(m),
            remote(n),
            remote(m),
        ],
        compiler_params=pltpu.CompilerParams(collective_id=0, has_side_effects=True),
        name="forward_exchange",
    )(
        row_part.reshape(row_shape),
        column_part.reshape(column_shape),
        pool_part,
        xmode_weight,
        ymode_weight,
        coarse_weight,
        mix_fore,
    )

    row_back, column_back, pool_back, totals = pl.pallas_call(
        ffn_kernel,
        grid=(steps,),
        in_specs=[
            block_spec,
            whole(2 * MODES_X, columns, channels),
            column_spec,
            whole(width, coarse_rows, channels),
            whole(channels, hidden),
            whole(hidden, channels),
            whole(channels, hidden),
            xfore_spec,
            xback_spec,
            whole(*yfore.shape),
            whole(*yback.shape),
        ],
        out_specs=analysis_specs + [whole(channels, 2 * hidden)],
        out_shape=analysis_out + [f32(channels, 2 * hidden)],
        scratch_shapes=[pltpu.VMEM((columns // TILE, 2 * MODES_X * TILE, channels), low)],
        compiler_params=sequential,
        name="feed_forward",
    )(
        cotangent,
        row_full.reshape(2 * MODES_X, columns, channels),
        column_full.reshape(2 * MODES_Y, rows, channels),
        coarse_own,
        lift_weight,
        lift_weight.T,
        drop_weight.T,
        xfore,
        xback,
        yfore,
        yback,
    )

    trows = channels // n
    xrows = 2 * modes * channels
    yrows = 2 * MODES_Y * channels
    cell_grad, total_full, x_grad, y_grad, c_grad = pl.pallas_call(
        functools.partial(backward_kernel, n, m, scales),
        out_shape=[
            jax.ShapeDtypeStruct(cells.shape, low),
            f32(channels, 2 * hidden),
            f32(xrows, channels),
            f32(yrows, channels),
            f32(channels, 2 * channels),
        ],
        in_specs=[VMEM_SPEC] * 14,
        out_specs=[VMEM_SPEC] * 5,
        scratch_shapes=[
            vm(n - 1, 2, modes, columns, channels),
            vm(m - 1, 2, MODES_Y, row_share, channels),
            vm(*row_shape),
            vm(*column_shape),
            vm(total_width, coarse_rows, channels),
            vm(total_width, coarse_rows, channels),
            vm(width, coarse_rows, channels),
            vm(n - 1, trows, 2 * hidden),
            vm(m, trows, 2 * hidden),
            vm(xrows, channels),
            vm(m - 1, xrows // m, channels),
            vm(yrows, channels),
            vm(n - 1, yrows // n, channels),
            vm(yrows // n, channels),
            vm(m - 1, yrows // n // m, channels),
            vm(channels, 2 * channels),
            vm(n - 1, trows, 2 * channels),
            pltpu.VMEM((columns // TILE, 2 * MODES_X * TILE, channels), low),
            remote(n),
            remote(m),
            remote(m),
            remote(n),
            remote(m),
            remote(n),
            remote(m),
            remote(n),
            remote(m),
            remote(m),
            remote(n),
            remote(m),
            remote(m),
            remote(n),
            remote(n),
            remote(n),
        ],
        compiler_params=pltpu.CompilerParams(collective_id=1, has_side_effects=True),
        name="backward_exchange",
    )(
        cotangent,
        row_back.reshape(row_shape),
        column_back.reshape(column_shape),
        pool_back,
        totals,
        row_own,
        column_own,
        pooled,
        xmode_weight,
        ymode_weight,
        coarse_weight,
        mix_back,
        xfore,
        yfore,
    )
    return (
        cell_grad,
        total_full[:, :hidden],
        total_full[:, hidden:].T,
        x_grad.reshape(2, modes, channels, channels),
        y_grad.reshape(2, MODES_Y, channels, channels),
        c_grad[:, :channels],
        c_grad[:total_width, channels : channels + total_width],
    )


def solution(mesh):
    in_specs = (
        P("gx", "gy", None),
        P("gx", "gy", None),
        P(),
        P(),
        P(None, "gx", None, None),
        P(),
        P(),
        P(),
    )
    out_specs = (P("gx", "gy", None), P(), P(), P(None, "gx", None, None), P(), P(), P())
    return jax.shard_map(
        functools.partial(on_device, mesh.shape["gx"], mesh.shape["gy"]),
        mesh=mesh,
        in_specs=in_specs,
        out_specs=out_specs,
        check_vma=False,
    )
```

time: 484 us -> 223 us (0.46); the launches traced: 477 us -> 223 us
  waiting for transfers between devices: 287 us -> 0 us
  Pallas kernels: 0 us -> 200 us
  matrix products: 98.1 us -> 9.83 us
  blocking collectives: 35.2 us -> 0 us
  local copies, waits for them, and re-layouts: 31.6 us -> 12.3 us
  between operations: 17.2 us -> 0.78 us
  other arithmetic: 7.65 us -> 0.08 us
    pallas_call x0 -> x4, Pallas kernels: none -> 200 us  [the longest x1 94.8 us: on_device(): pl.pallas_call(functools.partial(backward_kernel, n, m, scales), out_shap...]
    psum x2 -> x0, waiting for transfers between devices: 150 us -> none  [the longest x1 140 us: on_device(): lax.psum((lift_partial, drop_partial, column_weight_partial), ('gx', 'gy'))]
    unnamed x12 -> x0, waiting for transfers between devices: 109 us -> none
    dot_general x43 -> x6, matrix products: 98.1 us -> 9.83 us  [dot(): return jnp.dot(former, latter, preferred_element_type=wide)]
    all_gather x4 -> x0, waiting for transfers between devices: 28.4 us -> none  [the longest x2 21.8 us: column_return(): return lax.all_gather(owned_spec, 'gy', axis=2, tiled=True)]
    all_gather x2 -> x0, blocking collectives: 21.2 us -> none  [coarse_columns(): return lax.all_gather(coarse_block, 'gy', axis=1, tiled=True)]
    unnamed x46 -> x16, local copies, waits for them, and re-layouts: 23 us -> 7.74 us
    psum x1 -> x0, blocking collectives: 14 us -> none  [on_device(): lax.psum((coarse_weight_partial, mixing_partial), 'gx')]
  transfers between devices with their start and end apart: 10 -> 0, of which waited for: 6 -> 0; matrix products, arithmetic and copies ran while one was open for 17% -> 0% of each run, Pallas kernels for 0% -> 0%
where the time goes in v1:
time: 223 us
  Pallas kernels  200 us (90%)
  local copies, waits for them, and re-layouts  12.3 us (6%)
  matrix products  9.83 us (4%)
    pallas_call x1, Pallas kernels, on_device(): pl.pallas_call(functools.partial(backward_kernel, n, m, scales), out_shap...  94.8 us
    pallas_call x1, Pallas kernels, on_device(): pl.pallas_call(functools.partial(forward_kernel, n, m, scales), out_shape...  51 us
    pallas_call x1, Pallas kernels, on_device(): pl.pallas_call(ffn_kernel, grid=(steps,), in_specs=[block_spec, whole(2 *...  37.8 us
    pallas_call x1, Pallas kernels, on_device(): pl.pallas_call(analysis_kernel, grid=(steps,), in_specs=[block_spec, xbac...  16.2 us
    dot_general x6, matrix products, dot(): return jnp.dot(former, latter, preferred_element_type=wide)  9.83 us
    unnamed x16, local copies, waits for them, and re-layouts  7.74 us

profile of v1, /device:TPU:1, one launch (start us, length us, event | category | flops | bytes accessed | tf_op | source)
XLA Modules:
  0.0 222.7 jit_solution(1131414667916914862)
XLA Ops:
  0.6 0.0 copy-start
  0.6 0.0 copy-start.2
  0.7 0.0 copy-start.4
  0.8 0.5 copy-done
  1.3 0.9 fusion.5.mixrows_ref
  2.2 1.0 fusion.4.mixback_ref
  3.2 1.7 fusion.2.yback_ref
  4.9 1.8 fusion.3.yfore_ref
  6.8 0.0 copy-done.4
  6.8 0.8 copy.18
  7.5 0.8 copy.17
  8.3 2.0 fusion.xback_ref
  10.3 2.4 %fusion.1.xfore_ref = bf16[1024,256]{1,0:T(8,128)(2,1)} fusion(s32[256]{0:T(256)S(1)} %get-tuple-element.65, s32[256]{0:T(256)S(1)} %get-tuple-element.66, s32[1024]{0:T(1024)S(1)} %get-tuple-element.59, s32[1024]{0:T(1024)S(1)} %get-tuple-element.60, pred[1024]{0:T(1024)(128)(4,1)S(1)} %get-tuple-element.63, pred[256]{0:T(512)(128)(4,1)S(1)} %get-tuple-element.57, ...), kind=kOutput, calls=%fused_computation.3 | convolution fusion | flops 26787840 | bytes 555524 | tf_op jit(solution)/shard_map/dot_general | solution.py:34
  12.7 16.2 %analysis.1 = (f32[32,64,128]{2,1,0:T(8,128)}, f32[16,128,128]{2,1,0:T(8,128)}, f32[4,8,128]{2,1,0:T(8,128)}) custom-call(bf16[128,64,128]{2,1,0:T(8,128)(2,1)} %cells_ref.1, bf16[256,1024]{1,0:T(8,128)(2,1)} %fusion.xback_ref, bf16[128,512]{1,0:T(8,128)(2,1)} %fusion.2.yback_ref), custom_call_target="tpu_custom_call" | custom-call | tf_op jit(solution)/shard_map/analysis/pallas_call | solution.py:680
  28.9 51.0 %forward_exchange.1 = (f32[2,2,64,128]{3,2,1,0:T(8,128)}, f32[2,8,32,128]{3,2,1,0:T(8,128)}, f32[2,16,64,128]{3,2,1,0:T(8,128)}, f32[2,8,128,128]{3,2,1,0:T(8,12...) custom-call(f32[2,16,64,128]{3,2,1,0:T(8,128)} %bitcast.18, f32[2,8,128,128]{3,2,1,0:T(8,128)} %bitcast.19, ...), custom_call_target="tpu_custom_call" | custom-call | tf_op jit(solution)/shard_map/forward_exchange/pallas_call | solution.py:695
  79.9 37.8 %feed_forward.1 = (f32[32,64,128]{2,1,0:T(8,128)}, f32[16,128,128]{2,1,0:T(8,128)}, f32[4,8,128]{2,1,0:T(8,128)}, f32[128,1024]{1,0:T(8,128)}) custom-call(bf16[128,64,128]{2,1,0:T(8,128)(2,1)} %cotangent_ref.3, f32[32,64,128]{2,1,0:T(8,128)} %bitcast.16, f32[16,128,128]{2,1,0:T(8,128)} %bitcast.17, f32[4,8,128]{2,1,0:T(8,128)} %get-tuple-element.30.coarse_ref, ...), custom_call_target="tpu_custom_call" | custom-call | tf_op jit(solution)/shard_map/feed_forward/pallas_call | solution.py:728
  117.7 94.8 %backward_exchange.1 = (bf16[128,64,128]{2,1,0:T(8,128)(2,1)}, f32[128,1024]{1,0:T(8,128)}, f32[512,128]{1,0:T(8,128)}, f32[2048,128]{1,0:T(8,128)}, f32[128,256]{1,0:T(8,128)}) custom-call(bf16[128,64,128]{2,1,0:T(8,128)(2,1)} %cotangent_ref.3, f32[2,16,64,128]{3,2,1,0:T(8,128)} %bitcast.13, f32[2,8,128,128]{3,2,1,0:T(8,128)} %bitcast.14, ...), custom_call_target="tpu_custom_call" | custom-call | tf_op jit(solution)/shard_map/backward_exchange/pallas_call | solution.py:766
  212.5 1.3 slice.15
  213.8 1.5 slice.14
  215.3 1.8 slice_bitcast_fusion
  217.0 0.8 copy.19
  217.9 3.2 %copy.23 = bf16[128,64,128]{2,1,0:T(8,128)(2,1)} copy(bf16[128,64,128]{2,1,0:T(8,128)(2,1)} %get-tuple-element.89) | data formatting | bytes 4194304
  221.0 0.7 copy.24
  221.8 1.0 copy.25
  (20 shorter events, 0.1 us)
Async XLA Ops:
  0.6 0.7 copy-start
  0.6 6.9 %copy-start.2 = (bf16[128,512]{1,0:T(8,128)(2,1)S(1)}, bf16[128,512]{1,0:T(8,128)(2,1)}, u32[]{:S(2)}) copy-start(bf16[128,512]{1,0:T(8,128)(2,1)} %lift_ref.1) | copy-start | bytes 393220
  0.7 6.1 %copy-start.4 = (bf16[512,128]{1,0:T(8,128)(2,1)S(1)}, bf16[512,128]{1,0:T(8,128)(2,1)}, u32[]{:S(2)}) copy-start(bf16[512,128]{1,0:T(8,128)(2,1)} %param.13) | copy-start | bytes 393220
  217.9 3.2 %copy-start.3 = (f32[512,128]{1,0:T(8,128)S(1)}, f32[512,128]{1,0:T(8,128)}, u32[]{:S(2)}) copy-start(f32[512,128]{1,0:T(8,128)} %get-tuple-element.40) | copy-start | bytes 786436
  217.9 3.9 %copy-start.1 = (f32[2048,128]{1,0:T(8,128)S(1)}, f32[2048,128]{1,0:T(8,128)}, u32[]{:S(2)}) copy-start(f32[2048,128]{1,0:T(8,128)} %get-tuple-element.41) | copy-start | bytes 3145732

commit v2 on v1

--- a/solution.py
+++ b/solution.py
@@ -42,6 +42,25 @@
     return lax.dot_general(former, latter, (((0,), (0,)), ((), ())), preferred_element_type=wide)
 
 
+def halves(values):
+    high = values.astype(low)
+    return high, (values - high.astype(wide)).astype(low)
+
+
+def dot_fine(former, latter):
+    return sum(dot(part, latter) for part in halves(former))
+
+
+def dot_nt_fine(former, latter):
+    return sum(dot_nt(part, latter) for part in halves(former))
+
+
+def dot_tn_fine(former, latter):
+    high, rest = halves(former)
+    other, other_rest = halves(latter)
+    return dot_tn(high, other) + dot_tn(high, other_rest) + dot_tn(rest, other)
+
+
 def basis_table(mode_count, length):
     phase = np.outer(np.arange(mode_count), np.arange(length)) % length
     angles = phase * (2.0 * math.pi / length)
@@ -50,25 +69,35 @@
 
 def analyse(block, first, step, xback_ref, yback_ref, row_ref, column_ref, pool_ref):
     rows, columns, channels = block.shape
-    for tile in range(columns // TILE):
-        own = pl.ds(tile * TILE, TILE)
-        piece = block[:, tile * TILE : (tile + 1) * TILE, :].reshape(rows * TILE, channels)
-        part = dot(xback_ref[...], piece.astype(low)).reshape(2 * MODES_X, TILE, channels)
-
-        @pl.when(first)
-        def _():
-            row_ref[:, own, :] = part
-
-        @pl.when(jnp.logical_not(first))
-        def _():
-            row_ref[:, own, :] += part
-
-    for tile in range(rows // TILE):
-        piece = block[tile * TILE : (tile + 1) * TILE].reshape(TILE * columns, channels)
-        part = dot(yback_ref[...], piece.astype(low))
-        column_ref[:, tile * TILE : (tile + 1) * TILE, :] = part.reshape(
-            2 * MODES_Y, TILE, channels
-        )
+    for pair in range(columns // TILE // 2):
+        sides = []
+        for tile in (2 * pair, 2 * pair + 1):
+            piece = block[:, tile * TILE : (tile + 1) * TILE, :]
+            sides.append(piece.reshape(rows * TILE, channels).astype(low))
+        part = dot(xback_ref[...], jnp.concatenate(sides, axis=1))
+        for side in range(2):
+            own = pl.ds((2 * pair + side) * TILE, TILE)
+            mine = part[:, side * channels : (side + 1) * channels]
+            mine = mine.reshape(2 * MODES_X, TILE, channels)
+
+            @pl.when(first)
+            def _():
+                row_ref[:, own, :] = mine
+
+            @pl.when(jnp.logical_not(first))
+            def _():
+                row_ref[:, own, :] += mine
+
+    for pair in range(rows // TILE // 2):
+        sides = []
+        for tile in (2 * pair, 2 * pair + 1):
+            piece = block[tile * TILE : (tile + 1) * TILE].reshape(TILE * columns, channels)
+            sides.append(piece.astype(low))
+        part = dot(yback_ref[...], jnp.concatenate(sides, axis=1))
+        for side in range(2):
+            own = pl.ds((2 * pair + side) * TILE, TILE)
+            mine = part[:, side * channels : (side + 1) * channels]
+            column_ref[:, own, :] = mine.reshape(2 * MODES_Y, TILE, channels)
     pooled = block.sum(axis=0).reshape(columns // POOL, POOL, channels).sum(axis=1)
     pool_ref[:, pl.ds(step, 1), :] = pooled[:, None, :]
 
@@ -81,15 +110,31 @@
 
 def synthesise(rows, columns, channels, xfore, yfore_ref, row_low, column_of, coarse_of):
     parts = []
-    for tile in range(rows // TILE):
-        modes = column_of(tile).reshape(2 * MODES_Y * TILE, channels).astype(low)
-        parts.append(dot(yfore_ref[...], modes).reshape(TILE, columns, channels))
+    for pair in range(rows // TILE // 2):
+        sides = []
+        for tile in (2 * pair, 2 * pair + 1):
+            modes = column_of(tile).reshape(2 * MODES_Y * TILE, channels)
+            sides.append(modes.astype(low))
+        both = dot(yfore_ref[...], jnp.concatenate(sides, axis=1))
+        for side in range(2):
+            mine = both[:, side * channels : (side + 1) * channels]
+            parts.append(mine.reshape(TILE, columns, channels))
     field = jnp.concatenate(parts, axis=0)
     pieces = []
+    for pair in range(columns // TILE // 2):
+        both = dot(xfore, row_low(pair))
+        for side in range(2):
+            mine = both[:, side * channels : (side + 1) * channels]
+            part = mine.reshape(rows, TILE, channels)
+            pieces.append(part + coarse_of((2 * pair + side) * TILE // POOL))
+    return field + jnp.concatenate(pieces, axis=1)
+
+
+def fill_low(low_ref, tile_of, columns, channels):
     for tile in range(columns // TILE):
-        part = dot(xfore, row_low(tile)).reshape(rows, TILE, channels)
-        pieces.append(part + coarse_of(tile * TILE // POOL))
-    return field + jnp.concatenate(pieces, axis=1)
+        lanes = slice(tile % 2 * channels, (tile % 2 + 1) * channels)
+        modes = tile_of(tile).reshape(2 * MODES_X * TILE, channels)
+        low_ref[tile // 2, :, lanes] = modes.astype(low)
 
 
 def ffn_kernel(
@@ -116,12 +161,12 @@
 
     @pl.when(step == 0)
     def _():
-        for tile in range(columns // TILE):
-            rowlow_ref[tile] = (
-                rowf_ref[:, tile * TILE : (tile + 1) * TILE, :]
-                .reshape(2 * MODES_X * TILE, channels)
-                .astype(low)
-            )
+        fill_low(
+            rowlow_ref,
+            lambda tile: rowf_ref[:, tile * TILE : (tile + 1) * TILE, :],
+            columns,
+            channels,
+        )
         total_ref[...] = jnp.zeros_like(total_ref)
 
     coarse = coarse_ref[:, pl.ds(step, 1), :]
@@ -131,7 +176,7 @@
         channels,
         xfore_ref[...],
         yfore_ref,
-        lambda tile: rowlow_ref[tile],
+        lambda pair: rowlow_ref[pair],
         lambda tile: colf_ref[:, tile * TILE : (tile + 1) * TILE, :],
         lambda place: coarse[place : place + 1],
     )
@@ -246,9 +291,9 @@
     spec = sum_slots(rowp_ref[:, share(px, modes)], rowslots) * scale_rows
     rowown_ref[...] = spec
     for mode in range(modes):
-        both = spec[:, mode].reshape(2 * columns, channels).astype(low)
-        one = dot(both, xweight_ref[0, mode])
-        two = dot(both, xweight_ref[1, mode])
+        both = spec[:, mode].reshape(2 * columns, channels)
+        one = dot_fine(both, xweight_ref[0, mode])
+        two = dot_fine(both, xweight_ref[1, mode])
         gain = 1.0 / math.sqrt(MODES_X)
         rowf_ref[0, px * modes + mode] = (one[:columns] - two[columns:]) * gain
         rowf_ref[1, px * modes + mode] = (two[:columns] + one[columns:]) * gain
@@ -267,9 +312,9 @@
             spec = spec + colslots[k, :, mode]
         spec = spec * scale_columns
         colown_ref[:, mode] = spec
-        both = spec.reshape(2 * rows, channels).astype(low)
-        one = dot(both, yweight_ref[0, mode])
-        two = dot(both, yweight_ref[1, mode])
+        both = spec.reshape(2 * rows, channels)
+        one = dot_fine(both, yweight_ref[0, mode])
+        two = dot_fine(both, yweight_ref[1, mode])
         gain = 1.0 / math.sqrt(MODES_Y)
         colf_ref[0, mode, share(py, rows)] = (one[:rows] - two[rows:]) * gain
         colf_ref[1, mode, share(py, rows)] = (two[:rows] + one[rows:]) * gain
@@ -284,9 +329,9 @@
     arrive(to_pool)
     total_width, coarse_rows = pooled_ref.shape[:2]
     pooled = pooled_ref[...].reshape(total_width * coarse_rows, channels) * (1.0 / POOL)
-    pre = dot(pooled.astype(low), cweight_ref[...])
+    pre = dot_fine(pooled, cweight_ref[...])
     act, _ = gelu_pair(pre)
-    coarse_ref[...] = dot(mixrows_ref[...], act.astype(low)).reshape(coarse_ref.shape)
+    coarse_ref[...] = sum(dot(mixrows_ref[...], part) for part in halves(act)).reshape(coarse_ref.shape)
 
     arrive(to_rowf)
     arrive(to_colf)
@@ -377,13 +422,13 @@
     arrive(to_pool)
     total_width = grads_ref.shape[0]
     count = total_width * coarse_rows
-    pooled = (pooled_ref[...].reshape(count, channels) * (1.0 / POOL)).astype(low)
-    pre = dot(pooled, cweight_ref[...])
+    pooled = pooled_ref[...].reshape(count, channels) * (1.0 / POOL)
+    pre = dot_fine(pooled, cweight_ref[...])
     act, slope = gelu_pair(pre)
     grads = grads_ref[...].reshape(count, channels).astype(low)
     pre_grad = dot(mixback_ref[...], grads) * slope
     pregrad_ref[...] = pre_grad.reshape(pregrad_ref.shape)
-    cpart[:, 0:channels] = dot_tn(pooled, pre_grad.astype(low))
+    cpart[:, 0:channels] = dot_tn_fine(pooled, pre_grad)
     cross = dot_nt(grads, act.astype(low))
     left = lax.broadcasted_iota(jnp.int32, (count, count), 0) % coarse_rows
     right = lax.broadcasted_iota(jnp.int32, (count, count), 1) % coarse_rows
@@ -400,17 +445,15 @@
     crows = cpart.shape[0] // n
     to_c = send("gx", n, lambda d: cpart.at[share(d, crows)], lambda k: cslots.at[k], sem_c)
     own_grad = pregrad_ref[share(py, width)].reshape(width * coarse_rows, channels)
-    poolgrad_ref[...] = (dot_nt(own_grad.astype(low), cweight_ref[...]) * (1.0 / POOL)).reshape(
+    poolgrad_ref[...] = (dot_nt_fine(own_grad, cweight_ref[...]) * (1.0 / POOL)).reshape(
         poolgrad_ref.shape
     )
 
     def mix_back(spec, grad, real_weight, imaginary_weight):
         half_rows = spec.shape[0] // 2
-        grad_low = grad.astype(low)
-        turned = jnp.concatenate([grad[half_rows:], -grad[:half_rows]], axis=0).astype(low)
-        spec_low = spec.astype(low)
-        back = dot_nt(grad_low, real_weight) + dot_nt(turned, imaginary_weight)
-        return dot_tn(spec_low, grad_low), dot_tn(spec_low, turned), back
+        turned = jnp.concatenate([grad[half_rows:], -grad[:half_rows]], axis=0)
+        back = dot_nt_fine(grad, real_weight) + dot_nt_fine(turned, imaginary_weight)
+        return dot_tn_fine(spec, grad), dot_tn_fine(spec, turned), back
 
     arrive(to_row)
     grad = sum_slots(rowp_ref[:, share(px, modes)], rowslots) * (1.0 / math.sqrt(MODES_X))
@@ -490,7 +533,7 @@
             channels,
             xfore,
             yfore_ref,
-            lambda tile: rowlow_ref[tile],
+            lambda pair: rowlow_ref[pair],
             column_of,
             lambda place: coarse[place : place + 1],
         )
@@ -498,12 +541,12 @@
         cell_ref[own] = (cotangent_ref[own].astype(wide) + got).astype(low)
 
     arrive(to_rowf)
-    for tile in range(columns // TILE):
-        rowlow_ref[tile] = (
-            rowf_ref[:, :, tile * TILE : (tile + 1) * TILE, :]
-            .reshape(2 * MODES_X * TILE, channels)
-            .astype(low)
-        )
+    fill_low(
+        rowlow_ref,
+        lambda tile: rowf_ref[:, :, tile * TILE : (tile + 1) * TILE, :],
+        columns,
+        channels,
+    )
     arrive(to_y)
     ychunk[...] = sum_slots(ypart[share(px, yrows)], yslots)
     ycrows = yrows // m
@@ -743,7 +786,7 @@
         ],
         out_specs=analysis_specs + [whole(channels, 2 * hidden)],
         out_shape=analysis_out + [f32(channels, 2 * hidden)],
-        scratch_shapes=[pltpu.VMEM((columns // TILE, 2 * MODES_X * TILE, channels), low)],
+        scratch_shapes=[pltpu.VMEM((columns // TILE // 2, 2 * MODES_X * TILE, 2 * channels), low)],
         compiler_params=sequential,
         name="feed_forward",
     )(
@@ -792,7 +835,7 @@
             vm(m - 1, yrows // n // m, channels),
             vm(channels, 2 * channels),
             vm(n - 1, trows, 2 * channels),
-            pltpu.VMEM((columns // TILE, 2 * MODES_X * TILE, channels), low),
+            pltpu.VMEM((columns // TILE // 2, 2 * MODES_X * TILE, 2 * channels), low),
             remote(n),
             remote(m),
             remote(m),

time: 223 us -> 214 us (0.960)
  Pallas kernels: 200 us -> 191 us
    pallas_call x1, Pallas kernels: 37.8 us -> 33.3 us  [on_device(): pl.pallas_call(ffn_kernel, grid=(steps,), in_specs=[block_spec, whole(2 *...]
    pallas_call x1, Pallas kernels: 16.2 us -> 11.8 us  [on_device(): pl.pallas_call(analysis_kernel, grid=(steps,), in_specs=[block_spec, xbac...]
where the time goes in v2:
time: 214 us
  Pallas kernels  191 us (89%)
  local copies, waits for them, and re-layouts  12.3 us (6%)
  matrix products  9.83 us (5%)
    pallas_call x1, Pallas kernels, on_device(): pl.pallas_call(functools.partial(backward_kernel, n, m, scales), out_shap...  94.6 us
    pallas_call x1, Pallas kernels, on_device(): pl.pallas_call(functools.partial(forward_kernel, n, m, scales), out_shape...  51 us
    pallas_call x1, Pallas kernels, on_device(): pl.pallas_call(ffn_kernel, grid=(steps,), in_specs=[block_spec, whole(2 *...  33.3 us
    pallas_call x1, Pallas kernels, on_device(): pl.pallas_call(analysis_kernel, grid=(steps,), in_specs=[block_spec, xbac...  11.8 us
    dot_general x6, matrix products, dot(): return jnp.dot(former, latter, preferred_element_type=wide)  9.83 us
    unnamed x16, local copies, waits for them, and re-layouts  7.74 us

profile of v2, /device:TPU:1, one launch (start us, length us, event | category | flops | bytes accessed | tf_op | source)
XLA Modules:
  0.0 213.7 jit_solution(8864577332853686201)
XLA Ops:
  0.6 0.0 copy-start
  0.6 0.0 copy-start.2
  0.7 0.0 copy-start.4
  0.8 0.5 copy-done
  1.3 0.9 fusion.5.mixrows_ref
  2.2 1.0 fusion.4.mixback_ref
  3.2 1.7 fusion.2.yback_ref
  4.9 1.8 fusion.3.yfore_ref
  6.8 0.0 copy-done.4
  6.8 0.8 copy.18
  7.5 0.8 copy.17
  8.3 2.0 fusion.xback_ref
  10.3 2.4 %fusion.1.xfore_ref = bf16[1024,256]{1,0:T(8,128)(2,1)} fusion(s32[256]{0:T(256)S(1)} %get-tuple-element.65, s32[256]{0:T(256)S(1)} %get-tuple-element.66, s32[1024]{0:T(1024)S(1)} %get-tuple-element.59, s32[1024]{0:T(1024)S(1)} %get-tuple-element.60, pred[1024]{0:T(1024)(128)(4,1)S(1)} %get-tuple-element.63, pred[256]{0:T(512)(128)(4,1)S(1)} %get-tuple-element.57, ...), kind=kOutput, calls=%fused_computation.3 | convolution fusion | flops 26787840 | bytes 555524 | tf_op jit(solution)/shard_map/dot_general | solution.py:34
  12.7 11.8 %analysis.1 = (f32[32,64,128]{2,1,0:T(8,128)}, f32[16,128,128]{2,1,0:T(8,128)}, f32[4,8,128]{2,1,0:T(8,128)}) custom-call(bf16[128,64,128]{2,1,0:T(8,128)(2,1)} %cells_ref.1, bf16[256,1024]{1,0:T(8,128)(2,1)} %fusion.xback_ref, bf16[128,512]{1,0:T(8,128)(2,1)} %fusion.2.yback_ref), custom_call_target="tpu_custom_call" | custom-call | tf_op jit(solution)/shard_map/analysis/pallas_call | solution.py:723
  24.5 51.0 %forward_exchange.1 = (f32[2,2,64,128]{3,2,1,0:T(8,128)}, f32[2,8,32,128]{3,2,1,0:T(8,128)}, f32[2,16,64,128]{3,2,1,0:T(8,128)}, f32[2,8,128,128]{3,2,1,0:T(8,12...) custom-call(f32[2,16,64,128]{3,2,1,0:T(8,128)} %bitcast.18, f32[2,8,128,128]{3,2,1,0:T(8,128)} %bitcast.19, ...), custom_call_target="tpu_custom_call" | custom-call | tf_op jit(solution)/shard_map/forward_exchange/pallas_call | solution.py:738
  75.5 33.3 %feed_forward.1 = (f32[32,64,128]{2,1,0:T(8,128)}, f32[16,128,128]{2,1,0:T(8,128)}, f32[4,8,128]{2,1,0:T(8,128)}, f32[128,1024]{1,0:T(8,128)}) custom-call(bf16[128,64,128]{2,1,0:T(8,128)(2,1)} %cotangent_ref.3, f32[32,64,128]{2,1,0:T(8,128)} %bitcast.16, f32[16,128,128]{2,1,0:T(8,128)} %bitcast.17, f32[4,8,128]{2,1,0:T(8,128)} %get-tuple-element.30.coarse_ref, ...), custom_call_target="tpu_custom_call" | custom-call | tf_op jit(solution)/shard_map/feed_forward/pallas_call | solution.py:771
  108.9 94.6 %backward_exchange.1 = (bf16[128,64,128]{2,1,0:T(8,128)(2,1)}, f32[128,1024]{1,0:T(8,128)}, f32[512,128]{1,0:T(8,128)}, f32[2048,128]{1,0:T(8,128)}, f32[128,256]{1,0:T(8,128)}) custom-call(bf16[128,64,128]{2,1,0:T(8,128)(2,1)} %cotangent_ref.3, f32[2,16,64,128]{3,2,1,0:T(8,128)} %bitcast.13, f32[2,8,128,128]{3,2,1,0:T(8,128)} %bitcast.14, ...), custom_call_target="tpu_custom_call" | custom-call | tf_op jit(solution)/shard_map/backward_exchange/pallas_call | solution.py:809
  203.5 1.3 slice.15
  204.8 1.5 slice.14
  206.3 1.8 slice_bitcast_fusion
  208.0 0.8 copy.19
  208.9 3.2 %copy.23 = bf16[128,64,128]{2,1,0:T(8,128)(2,1)} copy(bf16[128,64,128]{2,1,0:T(8,128)(2,1)} %get-tuple-element.89) | data formatting | bytes 4194304
  212.1 0.7 copy.24
  212.8 1.0 copy.25
  (20 shorter events, 0.1 us)
Async XLA Ops:
  0.6 0.7 copy-start
  0.6 6.9 %copy-start.2 = (bf16[128,512]{1,0:T(8,128)(2,1)S(1)}, bf16[128,512]{1,0:T(8,128)(2,1)}, u32[]{:S(2)}) copy-start(bf16[128,512]{1,0:T(8,128)(2,1)} %lift_ref.1) | copy-start | bytes 393220
  0.7 6.1 %copy-start.4 = (bf16[512,128]{1,0:T(8,128)(2,1)S(1)}, bf16[512,128]{1,0:T(8,128)(2,1)}, u32[]{:S(2)}) copy-start(bf16[512,128]{1,0:T(8,128)(2,1)} %param.13) | copy-start | bytes 393220
  208.9 3.2 %copy-start.3 = (f32[512,128]{1,0:T(8,128)S(1)}, f32[512,128]{1,0:T(8,128)}, u32[]{:S(2)}) copy-start(f32[512,128]{1,0:T(8,128)} %get-tuple-element.40) | copy-start | bytes 786436
  208.9 3.9 %copy-start.1 = (f32[2048,128]{1,0:T(8,128)S(1)}, f32[2048,128]{1,0:T(8,128)}, u32[]{:S(2)}) copy-start(f32[2048,128]{1,0:T(8,128)} %get-tuple-element.41) | copy-start | bytes 3145732

commit v3 on v2

--- a/solution.py
+++ b/solution.py
@@ -13,6 +13,7 @@
 MODES_Y = 8
 POOL = 16
 TILE = 8
+PIECES = 4
 
 gelu_scale = 0.7978845608028654
 gelu_cubic = 0.044715
@@ -242,6 +243,110 @@
 
 def share(index, extent):
     return pl.ds(pl.multiple_of(index * extent, extent), extent)
+
+
+def gy_chain(m, part_ref, slots, full_ref, sem_sum, sem_back, mix_piece, between):
+    place = lax.axis_index("gy")
+    count = slots.shape[1]
+    extent = slots.shape[4]
+    half = count * extent
+    last = m - 1
+    end = (place == 0) | (place == last)
+
+    def piece(side, index):
+        begin = side * half + index * extent
+        if not isinstance(begin, int):
+            begin = pl.multiple_of(begin, extent)
+        return pl.ds(begin, extent)
+
+    def forth(side, index, source, dest):
+        return pltpu.make_async_remote_copy(
+            src_ref=source,
+            dst_ref=slots.at[side, index],
+            send_sem=sem_sum.at[0, side, index],
+            recv_sem=sem_sum.at[1, side, index],
+            device_id={"gy": dest},
+            device_id_type=MESH,
+        )
+
+    def back(side, index, dest):
+        return pltpu.make_async_remote_copy(
+            src_ref=full_ref.at[:, :, piece(side, index)],
+            dst_ref=full_ref.at[:, :, piece(side, index)],
+            send_sem=sem_back.at[0, side, index],
+            recv_sem=sem_back.at[1, side, index],
+            device_id={"gy": dest},
+            device_id_type=MESH,
+        )
+
+    other = lax.rem(place + 1, m)
+    for side in range(2):
+        begin = last if side == 0 else 0
+
+        @pl.when(place == begin)
+        def _():
+            for index in range(count):
+                forth(
+                    side,
+                    index,
+                    part_ref.at[:, :, piece(side, index)],
+                    last - 1 if side == 0 else 1,
+                ).start()
+
+    lag = 3
+    for turn in range(count + lag):
+        if turn < count:
+
+            @pl.when(jnp.logical_not(end))
+            def _():
+                for side in (1, 0):
+                    forth(side, turn, slots.at[side, turn], other).wait_recv()
+                    slots[side, turn] += part_ref[:, :, piece(side, turn)]
+                    dest = place + 1 if side else place - 1
+                    forth(side, turn, slots.at[side, turn], dest).start()
+
+            @pl.when(end)
+            def _():
+                side = place // last
+                forth(side, turn, slots.at[side, turn], other).wait_recv()
+                mix_piece(side, turn, piece(side, turn))
+                back(side, turn, 1 + side * (m - 3)).start()
+
+        if turn >= lag:
+
+            @pl.when(jnp.logical_not(end))
+            def _():
+                index = turn - lag
+                for side in (1, 0):
+                    back(side, index, other).wait_recv()
+                    dest = place - 1 if side else place + 1
+                    back(side, index, dest).start()
+
+        between(turn)
+
+    def finish():
+        for side in range(2):
+
+            @pl.when(place == (last if side == 0 else 0))
+            def _():
+                for index in range(count):
+                    back(side, index, other).wait_recv()
+
+    def settle():
+        for side in range(2):
+            final = 0 if side == 0 else last
+
+            @pl.when(place != final)
+            def _():
+                for index in range(count):
+                    forth(side, index, slots.at[side, index], other).wait_send()
+
+            @pl.when(place != last - final)
+            def _():
+                for index in range(count):
+                    back(side, index, other).wait_send()
+
+    return finish, settle
 
 
 def forward_kernel(
@@ -273,12 +378,8 @@
     px, py = lax.axis_index("gx"), lax.axis_index("gy")
     modes = MODES_X // n
     columns, channels = rowp_ref.shape[2:]
-    rows = colp_ref.shape[2] // m
     width = poolp_ref.shape[0]
     greet((("gx", n), ("gy", m)))
-    to_col = send(
-        "gy", m, lambda d: colp_ref.at[:, :, share(d, rows)], lambda k: colslots.at[k], sem_col
-    )
     to_row = send(
         "gx", n, lambda d: rowp_ref.at[:, share(d, modes)], lambda k: rowslots.at[k], sem_row
     )
@@ -287,43 +388,47 @@
     )
     pooled_ref[share(py, width)] = poolp_ref[...]
 
-    arrive(to_row)
-    spec = sum_slots(rowp_ref[:, share(px, modes)], rowslots) * scale_rows
-    rowown_ref[...] = spec
-    for mode in range(modes):
-        both = spec[:, mode].reshape(2 * columns, channels)
-        one = dot_fine(both, xweight_ref[0, mode])
-        two = dot_fine(both, xweight_ref[1, mode])
-        gain = 1.0 / math.sqrt(MODES_X)
-        rowf_ref[0, px * modes + mode] = (one[:columns] - two[columns:]) * gain
-        rowf_ref[1, px * modes + mode] = (two[:columns] + one[columns:]) * gain
-    to_rowf = send(
-        "gx",
-        n,
-        lambda d: rowf_ref.at[:, share(px, modes)],
-        lambda k: rowf_ref.at[:, share(px, modes)],
-        sem_rowf,
-    )
-
-    arrive(to_col)
-    for mode in range(MODES_Y):
-        spec = colp_ref[:, mode, share(py, rows)]
-        for k in range(m - 1):
-            spec = spec + colslots[k, :, mode]
-        spec = spec * scale_columns
-        colown_ref[:, mode] = spec
-        both = spec.reshape(2 * rows, channels)
-        one = dot_fine(both, yweight_ref[0, mode])
-        two = dot_fine(both, yweight_ref[1, mode])
+    to_rowf = []
+
+    def mix_rows():
+        arrive(to_row)
+        spec = sum_slots(rowp_ref[:, share(px, modes)], rowslots) * scale_rows
+        rowown_ref[...] = spec
+        for mode in range(modes):
+            both = spec[:, mode].reshape(2 * columns, channels)
+            one = dot_fine(both, xweight_ref[0, mode])
+            two = dot_fine(both, xweight_ref[1, mode])
+            gain = 1.0 / math.sqrt(MODES_X)
+            rowf_ref[0, px * modes + mode] = (one[:columns] - two[columns:]) * gain
+            rowf_ref[1, px * modes + mode] = (two[:columns] + one[columns:]) * gain
+        to_rowf.extend(
+            send(
+                "gx",
+                n,
+                lambda d: rowf_ref.at[:, share(px, modes)],
+                lambda k: rowf_ref.at[:, share(px, modes)],
+                sem_rowf,
+            )
+        )
+
+    def mix_piece(side, turn, own):
+        extent = colslots.shape[4]
+        spec = (colslots[side, turn] + colp_ref[:, :, own]) * scale_columns
+        colown_ref[:, :, turn * extent : (turn + 1) * extent] = spec
         gain = 1.0 / math.sqrt(MODES_Y)
-        colf_ref[0, mode, share(py, rows)] = (one[:rows] - two[rows:]) * gain
-        colf_ref[1, mode, share(py, rows)] = (two[:rows] + one[rows:]) * gain
-    to_colf = send(
-        "gy",
-        m,
-        lambda d: colf_ref.at[:, :, share(py, rows)],
-        lambda k: colf_ref.at[:, :, share(py, rows)],
-        sem_colf,
+        for mode in range(MODES_Y):
+            both = spec[:, mode].reshape(2 * extent, channels)
+            one = dot_fine(both, yweight_ref[0, mode])
+            two = dot_fine(both, yweight_ref[1, mode])
+            colf_ref[0, mode, own] = (one[:extent] - two[extent:]) * gain
+            colf_ref[1, mode, own] = (two[:extent] + one[extent:]) * gain
+
+    def between(turn):
+        if turn == 1:
+            mix_rows()
+
+    finish, settle = gy_chain(
+        m, colp_ref, colslots, colf_ref, sem_col, sem_colf, mix_piece, between
     )
 
     arrive(to_pool)
@@ -334,8 +439,9 @@
     coarse_ref[...] = sum(dot(mixrows_ref[...], part) for part in halves(act)).reshape(coarse_ref.shape)
 
     arrive(to_rowf)
-    arrive(to_colf)
-    for copies in (to_row, to_col, to_pool, to_rowf, to_colf):
+    finish()
+    settle()
+    for copies in (to_row, to_pool, to_rowf):
         leave(copies)
 
 
@@ -366,6 +472,7 @@
     colslots,
     rowf_ref,
     colf_ref,
+    colgrad_ref,
     grads_ref,
     pregrad_ref,
     poolgrad_ref,
@@ -401,104 +508,129 @@
     px, py = lax.axis_index("gx"), lax.axis_index("gy")
     modes = MODES_X // n
     columns, channels = rowp_ref.shape[2:]
-    rows = colp_ref.shape[2] // m
     width, coarse_rows = poolp_ref.shape[:2]
     greet((("gx", n), ("gy", m)))
     to_pool = send(
         "gy", m, lambda d: poolp_ref, lambda k: grads_ref.at[share(py, width)], sem_pool
     )
-    to_col = send(
-        "gy", m, lambda d: colp_ref.at[:, :, share(d, rows)], lambda k: colslots.at[k], sem_col
-    )
     to_row = send(
         "gx", n, lambda d: rowp_ref.at[:, share(d, modes)], lambda k: rowslots.at[k], sem_row
     )
     trows = total_ref.shape[0] // n
-    to_t = send(
-        "gx", n, lambda d: total_ref.at[share(d, trows)], lambda k: totalslots.at[k], sem_t
-    )
     grads_ref[share(py, width)] = poolp_ref[...]
 
-    arrive(to_pool)
-    total_width = grads_ref.shape[0]
-    count = total_width * coarse_rows
-    pooled = pooled_ref[...].reshape(count, channels) * (1.0 / POOL)
-    pre = dot_fine(pooled, cweight_ref[...])
-    act, slope = gelu_pair(pre)
-    grads = grads_ref[...].reshape(count, channels).astype(low)
-    pre_grad = dot(mixback_ref[...], grads) * slope
-    pregrad_ref[...] = pre_grad.reshape(pregrad_ref.shape)
-    cpart[:, 0:channels] = dot_tn_fine(pooled, pre_grad)
-    cross = dot_nt(grads, act.astype(low))
-    left = lax.broadcasted_iota(jnp.int32, (count, count), 0) % coarse_rows
-    right = lax.broadcasted_iota(jnp.int32, (count, count), 1) % coarse_rows
-    cross = jnp.where(left == right, cross, 0.0)
-    pick = (
-        lax.broadcasted_iota(jnp.int32, (channels, count), 0)
-        == lax.broadcasted_iota(jnp.int32, (channels, count), 1) // coarse_rows
-    ).astype(wide)
-    highest = lax.Precision.HIGHEST
-    half = jnp.dot(pick, cross, precision=highest, preferred_element_type=wide)
-    cpart[:, channels : 2 * channels] = lax.dot_general(
-        half, pick, (((1,), (1,)), ((), ())), precision=highest, preferred_element_type=wide
-    )
+    to_c_list = []
     crows = cpart.shape[0] // n
-    to_c = send("gx", n, lambda d: cpart.at[share(d, crows)], lambda k: cslots.at[k], sem_c)
-    own_grad = pregrad_ref[share(py, width)].reshape(width * coarse_rows, channels)
-    poolgrad_ref[...] = (dot_nt_fine(own_grad, cweight_ref[...]) * (1.0 / POOL)).reshape(
-        poolgrad_ref.shape
-    )
+
+    def coarse_level():
+        arrive(to_pool)
+        total_width = grads_ref.shape[0]
+        count = total_width * coarse_rows
+        pooled = pooled_ref[...].reshape(count, channels) * (1.0 / POOL)
+        pre = dot_fine(pooled, cweight_ref[...])
+        act, slope = gelu_pair(pre)
+        grads = grads_ref[...].reshape(count, channels).astype(low)
+        pre_grad = dot(mixback_ref[...], grads) * slope
+        pregrad_ref[...] = pre_grad.reshape(pregrad_ref.shape)
+        cpart[:, 0:channels] = dot_tn_fine(pooled, pre_grad)
+        cross = dot_nt(grads, act.astype(low))
+        left = lax.broadcasted_iota(jnp.int32, (count, count), 0) % coarse_rows
+        right = lax.broadcasted_iota(jnp.int32, (count, count), 1) % coarse_rows
+        cross = jnp.where(left == right, cross, 0.0)
+        pick = (
+            lax.broadcasted_iota(jnp.int32, (channels, count), 0)
+            == lax.broadcasted_iota(jnp.int32, (channels, count), 1) // coarse_rows
+        ).astype(wide)
+        highest = lax.Precision.HIGHEST
+        half = jnp.dot(pick, cross, precision=highest, preferred_element_type=wide)
+        cpart[:, channels : 2 * channels] = lax.dot_general(
+            half, pick, (((1,), (1,)), ((), ())), precision=highest, preferred_element_type=wide
+        )
+        to_c_list.extend(
+            send("gx", n, lambda d: cpart.at[share(d, crows)], lambda k: cslots.at[k], sem_c)
+        )
+        own_grad = pregrad_ref[share(py, width)].reshape(width * coarse_rows, channels)
+        poolgrad_ref[...] = (dot_nt_fine(own_grad, cweight_ref[...]) * (1.0 / POOL)).reshape(
+            poolgrad_ref.shape
+        )
+
+    def turn_modes(grad):
+        size = grad.shape[0] // 2
+        return grad, jnp.concatenate([grad[size:], -grad[:size]], axis=0)
 
     def mix_back(spec, grad, real_weight, imaginary_weight):
-        half_rows = spec.shape[0] // 2
-        turned = jnp.concatenate([grad[half_rows:], -grad[:half_rows]], axis=0)
+        grad, turned = turn_modes(grad)
         back = dot_nt_fine(grad, real_weight) + dot_nt_fine(turned, imaginary_weight)
         return dot_tn_fine(spec, grad), dot_tn_fine(spec, turned), back
 
-    arrive(to_row)
-    grad = sum_slots(rowp_ref[:, share(px, modes)], rowslots) * (1.0 / math.sqrt(MODES_X))
-    for mode in range(modes):
-        real, imaginary, back = mix_back(
-            rowown_ref[:, mode].reshape(2 * columns, channels),
-            grad[:, mode].reshape(2 * columns, channels),
-            xweight_ref[0, mode],
-            xweight_ref[1, mode],
+    to_rowf, to_t = [], []
+
+    def back_rows():
+        arrive(to_row)
+        grad = sum_slots(rowp_ref[:, share(px, modes)], rowslots) * (1.0 / math.sqrt(MODES_X))
+        for mode in range(modes):
+            real, imaginary, back = mix_back(
+                rowown_ref[:, mode].reshape(2 * columns, channels),
+                grad[:, mode].reshape(2 * columns, channels),
+                xweight_ref[0, mode],
+                xweight_ref[1, mode],
+            )
+            xpart[pl.ds(mode * channels, channels)] = real
+            xpart[pl.ds((modes + mode) * channels, channels)] = imaginary
+            rowf_ref[0, px * modes + mode] = back[:columns] * scale_rows
+            rowf_ref[1, px * modes + mode] = back[columns:] * scale_rows
+        to_rowf.extend(
+            send(
+                "gx",
+                n,
+                lambda d: rowf_ref.at[:, share(px, modes)],
+                lambda k: rowf_ref.at[:, share(px, modes)],
+                sem_rowf,
+            )
         )
-        xpart[pl.ds(mode * channels, channels)] = real
-        xpart[pl.ds((modes + mode) * channels, channels)] = imaginary
-        rowf_ref[0, px * modes + mode] = back[:columns] * scale_rows
-        rowf_ref[1, px * modes + mode] = back[columns:] * scale_rows
-    to_rowf = send(
-        "gx",
-        n,
-        lambda d: rowf_ref.at[:, share(px, modes)],
-        lambda k: rowf_ref.at[:, share(px, modes)],
-        sem_rowf,
-    )
-
-    arrive(to_col)
-    for mode in range(MODES_Y):
-        grad = colp_ref[:, mode, share(py, rows)]
-        for k in range(m - 1):
-            grad = grad + colslots[k, :, mode]
-        grad = grad * (1.0 / math.sqrt(MODES_Y))
-        real, imaginary, back = mix_back(
-            colown_ref[:, mode].reshape(2 * rows, channels),
-            grad.reshape(2 * rows, channels),
-            yweight_ref[0, mode],
-            yweight_ref[1, mode],
+        to_t.extend(
+            send(
+                "gx", n, lambda d: total_ref.at[share(d, trows)], lambda k: totalslots.at[k], sem_t
+            )
         )
-        ypart[pl.ds(mode * channels, channels)] = real
-        ypart[pl.ds((MODES_Y + mode) * channels, channels)] = imaginary
-        colf_ref[0, mode, share(py, rows)] = back[:rows] * scale_columns
-        colf_ref[1, mode, share(py, rows)] = back[rows:] * scale_columns
-    to_colf = send(
-        "gy",
-        m,
-        lambda d: colf_ref.at[:, :, share(py, rows)],
-        lambda k: colf_ref.at[:, :, share(py, rows)],
-        sem_colf,
-    )
+
+    extent = colslots.shape[4]
+
+    def mix_piece(side, turn, own):
+        grad = (colslots[side, turn] + colp_ref[:, :, own]) * (1.0 / math.sqrt(MODES_Y))
+        colgrad_ref[:, :, turn * extent : (turn + 1) * extent] = grad
+        for mode in range(MODES_Y):
+            both, turned = turn_modes(grad[:, mode].reshape(2 * extent, channels))
+            back = dot_nt_fine(both, yweight_ref[0, mode])
+            back = back + dot_nt_fine(turned, yweight_ref[1, mode])
+            colf_ref[0, mode, own] = back[:extent] * scale_columns
+            colf_ref[1, mode, own] = back[extent:] * scale_columns
+
+    def between(turn):
+        if turn == 0:
+            coarse_level()
+        if turn == 1:
+            back_rows()
+
+    finish, settle = gy_chain(
+        m, colp_ref, colslots, colf_ref, sem_col, sem_colf, mix_piece, between
+    )
+    to_c = to_c_list
+    owner = (py == 0) | (py == m - 1)
+
+    @pl.when(owner)
+    def _():
+        size = colown_ref.shape[2]
+        for mode in range(MODES_Y):
+            spec = colown_ref[:, mode].reshape(2 * size, channels)
+            grad, turned = turn_modes(colgrad_ref[:, mode].reshape(2 * size, channels))
+            ypart[pl.ds(mode * channels, channels)] = dot_tn_fine(spec, grad)
+            ypart[pl.ds((MODES_Y + mode) * channels, channels)] = dot_tn_fine(spec, turned)
+
+    @pl.when(jnp.logical_not(owner))
+    def _():
+        ypart[...] = jnp.zeros_like(ypart)
+
     yrows = ypart.shape[0] // n
     to_y = send("gx", n, lambda d: ypart.at[share(d, yrows)], lambda k: yslots.at[k], sem_y)
     xrows = xpart.shape[0] // m
@@ -572,7 +704,7 @@
         lambda k: totalf_ref.at[share(px, trows)],
         sem_tf,
     )
-    arrive(to_colf)
+    finish()
     steps = cell_ref.shape[0] // block
     early = steps // 2
 
@@ -597,16 +729,15 @@
     def _(step):
         field(step)
 
+    settle()
     for copies in (to_cf, to_xf, to_tf, to_yf):
         arrive(copies)
     for copies in (
         to_pool,
-        to_col,
         to_row,
         to_t,
         to_c,
         to_rowf,
-        to_colf,
         to_y,
         to_x,
         to_tg,
@@ -637,6 +768,10 @@
 
 def remote(size):
     return pltpu.SemaphoreType.DMA((2, size - 1))
+
+
+def chained():
+    return pltpu.SemaphoreType.DMA((2, 2, PIECES))
 
 
 def on_device(
@@ -657,7 +792,6 @@
     coarse_rows, width = rows // POOL, columns // POOL
     total_width = width * m
     modes = MODES_X // n
-    row_share = rows // m
     px, py = lax.axis_index("gx"), lax.axis_index("gy")
     row_basis = lax.dynamic_slice_in_dim(
         jnp.asarray(basis_table(MODES_X, row_total)), px * rows, rows, 1
@@ -739,7 +873,7 @@
         functools.partial(forward_kernel, n, m, scales),
         out_shape=[
             f32(2, modes, columns, channels),
-            f32(2, MODES_Y, row_share, channels),
+            f32(2, MODES_Y, rows // 2, channels),
             f32(*row_shape),
             f32(*column_shape),
             f32(total_width, coarse_rows, channels),
@@ -749,12 +883,12 @@
         out_specs=[VMEM_SPEC] * 6,
         scratch_shapes=[
             vm(n - 1, 2, modes, columns, channels),
-            vm(m - 1, 2, MODES_Y, row_share, channels),
+            vm(2, PIECES, 2, MODES_Y, rows // 2 // PIECES, channels),
             remote(n),
-            remote(m),
+            chained(),
             remote(m),
             remote(n),
-            remote(m),
+            chained(),
         ],
         compiler_params=pltpu.CompilerParams(collective_id=0, has_side_effects=True),
         name="forward_exchange",
@@ -819,9 +953,10 @@
         out_specs=[VMEM_SPEC] * 5,
         scratch_shapes=[
             vm(n - 1, 2, modes, columns, channels),
-            vm(m - 1, 2, MODES_Y, row_share, channels),
+            vm(2, PIECES, 2, MODES_Y, rows // 2 // PIECES, channels),
             vm(*row_shape),
             vm(*column_shape),
+            vm(2, MODES_Y, rows // 2, channels),
             vm(total_width, coarse_rows, channels),
             vm(total_width, coarse_rows, channels),
             vm(width, coarse_rows, channels),
@@ -837,10 +972,10 @@
             vm(n - 1, trows, 2 * channels),
             pltpu.VMEM((columns // TILE // 2, 2 * MODES_X * TILE, 2 * channels), low),
             remote(n),
-            remote(m),
+            chained(),
             remote(m),
             remote(n),
-            remote(m),
+            chained(),
             remote(n),
             remote(m),
             remote(n),

time: 214 us -> 271 us (1.27)
  Pallas kernels: 191 us -> 248 us
    pallas_call x1, Pallas kernels: 94.6 us -> 136 us  [on_device(): pl.pallas_call(functools.partial(backward_kernel, n, m, scales), out_shap...]
    pallas_call x1, Pallas kernels: 51 us -> 66.2 us  [on_device(): pl.pallas_call(functools.partial(forward_kernel, n, m, scales), out_shape...]
where the time goes in v3:
time: 271 us; the launch traced here: 270 us
  Pallas kernels  248 us (92%)
  local copies, waits for them, and re-layouts  12.3 us (5%)
  matrix products  9.81 us (4%)
    pallas_call x1, Pallas kernels, on_device(): pl.pallas_call(functools.partial(backward_kernel, n, m, scales), out_shap...  136 us
    pallas_call x1, Pallas kernels, on_device(): pl.pallas_call(functools.partial(forward_kernel, n, m, scales), out_shape...  66.2 us
    pallas_call x1, Pallas kernels, on_device(): pl.pallas_call(ffn_kernel, grid=(steps,), in_specs=[block_spec, whole(2 *...  33.4 us
    pallas_call x1, Pallas kernels, on_device(): pl.pallas_call(analysis_kernel, grid=(steps,), in_specs=[block_spec, xbac...  11.8 us
    dot_general x6, matrix products, dot(): return jnp.dot(former, latter, preferred_element_type=wide)  9.81 us
    unnamed x16, local copies, waits for them, and re-layouts  7.74 us

profile of v3, /device:TPU:1, one launch (start us, length us, event | category | flops | bytes accessed | tf_op | source)
XLA Modules:
  0.0 270.5 jit_solution(7449866937386904205)
XLA Ops:
  0.6 0.0 copy-start
  0.6 0.0 copy-start.2
  0.7 0.0 copy-start.4
  0.8 0.5 copy-done
  1.3 0.9 fusion.5.mixrows_ref
  2.2 1.0 fusion.4.mixback_ref
  3.2 1.7 fusion.2.yback_ref
  4.9 1.8 fusion.3.yfore_ref
  6.8 0.0 copy-done.4
  6.8 0.8 copy.18
  7.6 0.8 copy.17
  8.3 2.0 fusion.xback_ref
  10.3 2.4 fusion.1.xfore_ref
  12.7 11.8 %analysis.1 = (f32[32,64,128]{2,1,0:T(8,128)}, f32[16,128,128]{2,1,0:T(8,128)}, f32[4,8,128]{2,1,0:T(8,128)}) custom-call(bf16[128,64,128]{2,1,0:T(8,128)(2,1)} %cells_ref.1, bf16[256,1024]{1,0:T(8,128)(2,1)} %fusion.xback_ref, bf16[128,512]{1,0:T(8,128)(2,1)} %fusion.2.yback_ref), custom_call_target="tpu_custom_call" | custom-call | tf_op jit(solution)/shard_map/analysis/pallas_call | solution.py:857
  24.5 66.2 %forward_exchange.1 = (f32[2,2,64,128]{3,2,1,0:T(8,128)}, f32[2,8,64,128]{3,2,1,0:T(8,128)}, f32[2,16,64,128]{3,2,1,0:T(8,128)}, f32[2,8,128,128]{3,2,1,0:T(8,12...) custom-call(f32[2,16,64,128]{3,2,1,0:T(8,128)} %bitcast.18, f32[2,8,128,128]{3,2,1,0:T(8,128)} %bitcast.19, ...), custom_call_target="tpu_custom_call" | custom-call | tf_op jit(solution)/shard_map/forward_exchange/pallas_call | solution.py:872
  90.7 33.4 %feed_forward.1 = (f32[32,64,128]{2,1,0:T(8,128)}, f32[16,128,128]{2,1,0:T(8,128)}, f32[4,8,128]{2,1,0:T(8,128)}, f32[128,1024]{1,0:T(8,128)}) custom-call(bf16[128,64,128]{2,1,0:T(8,128)(2,1)} %cotangent_ref.3, f32[32,64,128]{2,1,0:T(8,128)} %bitcast.16, f32[16,128,128]{2,1,0:T(8,128)} %bitcast.17, f32[4,8,128]{2,1,0:T(8,128)} %get-tuple-element.30.coarse_ref, ...), custom_call_target="tpu_custom_call" | custom-call | tf_op jit(solution)/shard_map/feed_forward/pallas_call | solution.py:905
  124.0 136.2 %backward_exchange.1 = (bf16[128,64,128]{2,1,0:T(8,128)(2,1)}, f32[128,1024]{1,0:T(8,128)}, f32[512,128]{1,0:T(8,128)}, f32[2048,128]{1,0:T(8,128)}, f32[128,256]{1,0:T(8,128)}) custom-call(bf16[128,64,128]{2,1,0:T(8,128)(2,1)} %cotangent_ref.3, f32[2,16,64,128]{3,2,1,0:T(8,128)} %bitcast.14, f32[2,8,128,128]{3,2,1,0:T(8,128)} %bitcast.15, ...), custom_call_target="tpu_custom_call" | custom-call | tf_op jit(solution)/shard_map/backward_exchange/pallas_call | solution.py:943
  260.2 1.3 slice.15
  261.5 1.5 slice.14
  263.0 1.8 slice_bitcast_fusion
  264.8 0.8 copy.19
  265.6 3.2 %copy.23 = bf16[128,64,128]{2,1,0:T(8,128)(2,1)} copy(bf16[128,64,128]{2,1,0:T(8,128)(2,1)} %get-tuple-element.89) | data formatting | bytes 4194304
  268.8 0.7 copy.24
  269.5 1.0 copy.25
  (20 shorter events, 0.1 us)
Async XLA Ops:
  0.6 0.7 copy-start
  0.6 6.9 %copy-start.2 = (bf16[128,512]{1,0:T(8,128)(2,1)S(1)}, bf16[128,512]{1,0:T(8,128)(2,1)}, u32[]{:S(2)}) copy-start(bf16[128,512]{1,0:T(8,128)(2,1)} %lift_ref.1) | copy-start | bytes 393220
  0.7 6.1 %copy-start.4 = (bf16[512,128]{1,0:T(8,128)(2,1)S(1)}, bf16[512,128]{1,0:T(8,128)(2,1)}, u32[]{:S(2)}) copy-start(bf16[512,128]{1,0:T(8,128)(2,1)} %param.13) | copy-start | bytes 393220
  265.6 3.2 %copy-start.3 = (f32[512,128]{1,0:T(8,128)S(1)}, f32[512,128]{1,0:T(8,128)}, u32[]{:S(2)}) copy-start(f32[512,128]{1,0:T(8,128)} %get-tuple-element.40) | copy-start | bytes 786436
  265.6 3.9 %copy-start.1 = (f32[2048,128]{1,0:T(8,128)S(1)}, f32[2048,128]{1,0:T(8,128)}, u32[]{:S(2)}) copy-start(f32[2048,128]{1,0:T(8,128)} %get-tuple-element.41) | copy-start | bytes 3145732

commit v4 on v2

--- a/solution.py
+++ b/solution.py
@@ -254,13 +254,17 @@
     xweight_ref,
     yweight_ref,
     cweight_ref,
-    mixrows_ref,
+    mixall_ref,
+    xback_ref,
+    yback_ref,
     rowown_ref,
     colown_ref,
     rowf_ref,
     colf_ref,
     pooled_ref,
     coarse_ref,
+    xfore_ref,
+    yfore_ref,
     rowslots,
     colslots,
     sem_row,
@@ -286,6 +290,10 @@
         "gy", m, lambda d: poolp_ref, lambda k: pooled_ref.at[share(py, width)], sem_pool
     )
     pooled_ref[share(py, width)] = poolp_ref[...]
+    for back_ref, fore_ref in ((xback_ref, xfore_ref), (yback_ref, yfore_ref)):
+        for begin in range(0, back_ref.shape[1], channels):
+            part = back_ref[:, begin : begin + channels].astype(wide)
+            fore_ref[begin : begin + channels] = part.T.astype(low)
 
     arrive(to_row)
     spec = sum_slots(rowp_ref[:, share(px, modes)], rowslots) * scale_rows
@@ -331,7 +339,8 @@
     pooled = pooled_ref[...].reshape(total_width * coarse_rows, channels) * (1.0 / POOL)
     pre = dot_fine(pooled, cweight_ref[...])
     act, _ = gelu_pair(pre)
-    coarse_ref[...] = sum(dot(mixrows_ref[...], part) for part in halves(act)).reshape(coarse_ref.shape)
+    own_rows = mixall_ref[share(py, width * coarse_rows)]
+    coarse_ref[...] = sum(dot(own_rows, part) for part in halves(act)).reshape(coarse_ref.shape)
 
     arrive(to_rowf)
     arrive(to_colf)
@@ -354,7 +363,7 @@
     xweight_ref,
     yweight_ref,
     cweight_ref,
-    mixback_ref,
+    mixall_ref,
     xfore_ref,
     yfore_ref,
     cell_ref,
@@ -426,7 +435,7 @@
     pre = dot_fine(pooled, cweight_ref[...])
     act, slope = gelu_pair(pre)
     grads = grads_ref[...].reshape(count, channels).astype(low)
-    pre_grad = dot(mixback_ref[...], grads) * slope
+    pre_grad = dot_tn(mixall_ref[...], grads) * slope
     pregrad_ref[...] = pre_grad.reshape(pregrad_ref.shape)
     cpart[:, 0:channels] = dot_tn_fine(pooled, pre_grad)
     cross = dot_nt(grads, act.astype(low))
@@ -449,23 +458,24 @@
         poolgrad_ref.shape
     )
 
-    def mix_back(spec, grad, real_weight, imaginary_weight):
-        half_rows = spec.shape[0] // 2
-        turned = jnp.concatenate([grad[half_rows:], -grad[:half_rows]], axis=0)
-        back = dot_nt_fine(grad, real_weight) + dot_nt_fine(turned, imaginary_weight)
-        return dot_tn_fine(spec, grad), dot_tn_fine(spec, turned), back
+    def turn_modes(grad):
+        half_rows = grad.shape[0] // 2
+        return grad, jnp.concatenate([grad[half_rows:], -grad[:half_rows]], axis=0)
+
+    def weight_back(spec, grad):
+        grad, turned = turn_modes(grad)
+        return dot_tn_fine(spec, grad), dot_tn_fine(spec, turned)
+
+    def spec_back(grad, real_weight, imaginary_weight):
+        grad, turned = turn_modes(grad)
+        return dot_nt_fine(grad, real_weight) + dot_nt_fine(turned, imaginary_weight)
 
     arrive(to_row)
     grad = sum_slots(rowp_ref[:, share(px, modes)], rowslots) * (1.0 / math.sqrt(MODES_X))
     for mode in range(modes):
-        real, imaginary, back = mix_back(
-            rowown_ref[:, mode].reshape(2 * columns, channels),
-            grad[:, mode].reshape(2 * columns, channels),
-            xweight_ref[0, mode],
-            xweight_ref[1, mode],
+        back = spec_back(
+            grad[:, mode].reshape(2 * columns, channels), xweight_ref[0, mode], xweight_ref[1, mode]
         )
-        xpart[pl.ds(mode * channels, channels)] = real
-        xpart[pl.ds((modes + mode) * channels, channels)] = imaginary
         rowf_ref[0, px * modes + mode] = back[:columns] * scale_rows
         rowf_ref[1, px * modes + mode] = back[columns:] * scale_rows
     to_rowf = send(
@@ -475,21 +485,32 @@
         lambda k: rowf_ref.at[:, share(px, modes)],
         sem_rowf,
     )
+    for mode in range(modes):
+        real, imaginary = weight_back(
+            rowown_ref[:, mode].reshape(2 * columns, channels),
+            grad[:, mode].reshape(2 * columns, channels),
+        )
+        xpart[pl.ds(mode * channels, channels)] = real
+        xpart[pl.ds((modes + mode) * channels, channels)] = imaginary
 
     arrive(to_col)
+    grad = colp_ref[:, :, share(py, rows)]
+    for k in range(m - 1):
+        grad = grad + colslots[k]
+    grad = grad * (1.0 / math.sqrt(MODES_Y))
     for mode in range(MODES_Y):
-        grad = colp_ref[:, mode, share(py, rows)]
-        for k in range(m - 1):
-            grad = grad + colslots[k, :, mode]
-        grad = grad * (1.0 / math.sqrt(MODES_Y))
-        real, imaginary, back = mix_back(
+        real, imaginary = weight_back(
             colown_ref[:, mode].reshape(2 * rows, channels),
-            grad.reshape(2 * rows, channels),
-            yweight_ref[0, mode],
-            yweight_ref[1, mode],
+            grad[:, mode].reshape(2 * rows, channels),
         )
         ypart[pl.ds(mode * channels, channels)] = real
         ypart[pl.ds((MODES_Y + mode) * channels, channels)] = imaginary
+    yrows = ypart.shape[0] // n
+    to_y = send("gx", n, lambda d: ypart.at[share(d, yrows)], lambda k: yslots.at[k], sem_y)
+    for mode in range(MODES_Y):
+        back = spec_back(
+            grad[:, mode].reshape(2 * rows, channels), yweight_ref[0, mode], yweight_ref[1, mode]
+        )
         colf_ref[0, mode, share(py, rows)] = back[:rows] * scale_columns
         colf_ref[1, mode, share(py, rows)] = back[rows:] * scale_columns
     to_colf = send(
@@ -499,8 +520,6 @@
         lambda k: colf_ref.at[:, :, share(py, rows)],
         sem_colf,
     )
-    yrows = ypart.shape[0] // n
-    to_y = send("gx", n, lambda d: ypart.at[share(d, yrows)], lambda k: yslots.at[k], sem_y)
     xrows = xpart.shape[0] // m
     to_x = send("gy", m, lambda d: xpart.at[share(d, xrows)], lambda k: xslots.at[k], sem_x)
 
@@ -576,14 +595,14 @@
     steps = cell_ref.shape[0] // block
     early = steps // 2
 
-    @pl.loop(0, early)
-    def _(step):
-        field(step)
-
     arrive(to_yc)
     own_y = pl.ds(pl.multiple_of(px * yrows + py * ycrows, ycrows), ycrows)
     ygrad_ref[own_y] = sum_slots(ychunk[share(py, ycrows)], ycslots)
     to_ycf = send("gy", m, lambda d: ygrad_ref.at[own_y], lambda k: ygrad_ref.at[own_y], sem_ycf)
+    @pl.loop(0, early)
+    def _(step):
+        field(step)
+
     arrive(to_ycf)
     to_yf = send(
         "gx",
@@ -667,17 +686,8 @@
     ).astype(low)
     by_tile = lambda v: v // TILE
     same_tile = lambda r, c: r % TILE == c % TILE
-    xfore = spread(rows * TILE, 2 * MODES_X * TILE, by_tile, by_tile, row_basis.T, same_tile)
     xback = spread(2 * MODES_X * TILE, rows * TILE, by_tile, by_tile, row_basis, same_tile)
     in_columns = lambda v: v % columns
-    yfore = spread(
-        TILE * columns,
-        2 * MODES_Y * TILE,
-        in_columns,
-        by_tile,
-        column_basis.T,
-        lambda r, c: r // columns == c % TILE,
-    )
     yback = spread(
         2 * MODES_Y * TILE,
         TILE * columns,
@@ -688,16 +698,12 @@
     )
     by_coarse = lambda v: v // coarse_rows
     same_coarse = lambda r, c: r % coarse_rows == c % coarse_rows
-    mix_rows = lax.dynamic_slice_in_dim(coarse_mix, py * width, width, 0)
-    mix_fore = spread(
-        width * coarse_rows, total_width * coarse_rows, by_coarse, by_coarse, mix_rows, same_coarse
-    )
-    mix_back = spread(
+    mix_all = spread(
         total_width * coarse_rows,
         total_width * coarse_rows,
         by_coarse,
         by_coarse,
-        coarse_mix.T,
+        coarse_mix,
         same_coarse,
     )
     steps = rows // POOL
@@ -735,7 +741,7 @@
     column_shape = (2, MODES_Y, rows, channels)
     f32 = lambda *shape: jax.ShapeDtypeStruct(shape, wide)
     vm = lambda *shape: pltpu.VMEM(shape, wide)
-    row_own, column_own, row_full, column_full, pooled, coarse_own = pl.pallas_call(
+    row_own, column_own, row_full, column_full, pooled, coarse_own, xfore, yfore = pl.pallas_call(
         functools.partial(forward_kernel, n, m, scales),
         out_shape=[
             f32(2, modes, columns, channels),
@@ -744,9 +750,11 @@
             f32(*column_shape),
             f32(total_width, coarse_rows, channels),
             f32(width, coarse_rows, channels),
+            jax.ShapeDtypeStruct(xback.shape[::-1], low),
+            jax.ShapeDtypeStruct(yback.shape[::-1], low),
         ],
-        in_specs=[VMEM_SPEC] * 7,
-        out_specs=[VMEM_SPEC] * 6,
+        in_specs=[VMEM_SPEC] * 9,
+        out_specs=[VMEM_SPEC] * 8,
         scratch_shapes=[
             vm(n - 1, 2, modes, columns, channels),
             vm(m - 1, 2, MODES_Y, row_share, channels),
@@ -765,7 +773,9 @@
         xmode_weight,
         ymode_weight,
         coarse_weight,
-        mix_fore,
+        mix_all,
+        xback,
+        yback,
     )
 
     row_back, column_back, pool_back, totals = pl.pallas_call(
@@ -867,7 +877,7 @@
         xmode_weight,
         ymode_weight,
         coarse_weight,
-        mix_back,
+        mix_all,
         xfore,
         yfore,
     )

time: 214 us -> 211 us (0.986)
  matrix products: 9.83 us -> 4.67 us
    dot_general x6 -> x3, matrix products: 9.83 us -> 4.67 us  [dot(): return jnp.dot(former, latter, preferred_element_type=wide)]
    unnamed x16 -> x12, local copies, waits for them, and re-layouts: 7.74 us -> 9.56 us
where the time goes in v4:
time: 211 us
  Pallas kernels  191 us (91%)
  local copies, waits for them, and re-layouts  14.1 us (7%)
  matrix products  4.67 us (2%)
    pallas_call x1, Pallas kernels, on_device(): pl.pallas_call(functools.partial(backward_kernel, n, m, scales), out_shap...  94.6 us
    pallas_call x1, Pallas kernels, on_device(): pl.pallas_call(functools.partial(forward_kernel, n, m, scales), out_shape...  51.4 us
    pallas_call x1, Pallas kernels, on_device(): pl.pallas_call(ffn_kernel, grid=(steps,), in_specs=[block_spec, whole(2 *...  33.3 us
    pallas_call x1, Pallas kernels, on_device(): pl.pallas_call(analysis_kernel, grid=(steps,), in_specs=[block_spec, xbac...  11.8 us
    unnamed x12, local copies, waits for them, and re-layouts  9.56 us
    dot_general x3, matrix products, dot(): return jnp.dot(former, latter, preferred_element_type=wide)  4.67 us

profile of v4, /device:TPU:1, one launch (start us, length us, event | category | flops | bytes accessed | tf_op | source)
XLA Modules:
  0.0 210.8 jit_solution(1932885343798177099)
XLA Ops:
  0.6 0.0 copy-start
  0.8 0.5 copy-done
  1.3 1.0 fusion.2.mixall_ref
  2.3 1.7 fusion.1.yback_ref
  4.0 1.7 copy.18
  5.7 1.7 copy.17
  7.3 2.0 fusion.xback_ref
  9.3 11.8 %analysis.1 = (f32[32,64,128]{2,1,0:T(8,128)}, f32[16,128,128]{2,1,0:T(8,128)}, f32[4,8,128]{2,1,0:T(8,128)}) custom-call(bf16[128,64,128]{2,1,0:T(8,128)(2,1)} %cells_ref.1, bf16[256,1024]{1,0:T(8,128)(2,1)} %fusion.xback_ref, bf16[128,512]{1,0:T(8,128)(2,1)} %fusion.1.yback_ref), custom_call_target="tpu_custom_call" | custom-call | tf_op jit(solution)/shard_map/analysis/pallas_call | solution.py:729
  21.1 51.4 %forward_exchange.1 = (f32[2,2,64,128]{3,2,1,0:T(8,128)}, f32[2,8,32,128]{3,2,1,0:T(8,128)}, f32[2,16,64,128]{3,2,1,0:T(8,128)}, f32[2,8,128,128]{3,2,1,0:T(8,12...) custom-call(f32[2,16,64,128]{3,2,1,0:T(8,128)} %bitcast.16, ...), custom_call_target="tpu_custom_call" | custom-call | tf_op jit(solution)/shard_map/forward_exchange/pallas_call | solution.py:744
  72.5 33.3 %feed_forward.1 = (f32[32,64,128]{2,1,0:T(8,128)}, f32[16,128,128]{2,1,0:T(8,128)}, f32[4,8,128]{2,1,0:T(8,128)}, f32[128,1024]{1,0:T(8,128)}) custom-call(bf16[128,64,128]{2,1,0:T(8,128)(2,1)} %cotangent_ref.3, f32[32,64,128]{2,1,0:T(8,128)} %bitcast.18, f32[16,128,128]{2,1,0:T(8,128)} %bitcast.19, f32[4,8,128]{2,1,0:T(8,128)} %get-tuple-element.32.coarse_ref, ...), custom_call_target="tpu_custom_call" | custom-call | tf_op jit(solution)/shard_map/feed_forward/pallas_call | solution.py:781
  105.9 94.6 %backward_exchange.1 = (bf16[128,64,128]{2,1,0:T(8,128)(2,1)}, f32[128,1024]{1,0:T(8,128)}, f32[512,128]{1,0:T(8,128)}, f32[2048,128]{1,0:T(8,128)}, f32[128,256]{1,0:T(8,128)}) custom-call(bf16[128,64,128]{2,1,0:T(8,128)(2,1)} %cotangent_ref.3, f32[2,16,64,128]{3,2,1,0:T(8,128)} %bitcast.13, f32[2,8,128,128]{3,2,1,0:T(8,128)} %bitcast.14, ...), custom_call_target="tpu_custom_call" | custom-call | tf_op jit(solution)/shard_map/backward_exchange/pallas_call | solution.py:819
  200.5 1.3 slice.15
  201.8 1.5 slice.14
  203.3 1.8 slice_bitcast_fusion
  205.1 0.8 copy.19
  205.9 0.0 copy-start.2
  205.9 0.0 copy-start.1
  205.9 3.2 %copy.23 = bf16[128,64,128]{2,1,0:T(8,128)(2,1)} copy(bf16[128,64,128]{2,1,0:T(8,128)(2,1)} %get-tuple-element.87) | data formatting | bytes 4194304
  209.1 0.0 copy-done.2
  209.1 0.7 copy.24
  209.8 0.0 copy-done.1
  209.8 1.0 copy.25
  (12 shorter events, 0.1 us)
Async XLA Ops:
  0.6 0.7 copy-start
  205.9 3.2 %copy-start.2 = (f32[512,128]{1,0:T(8,128)S(1)}, f32[512,128]{1,0:T(8,128)}, u32[]{:S(2)}) copy-start(f32[512,128]{1,0:T(8,128)} %get-tuple-element.44) | copy-start | bytes 786436
  205.9 3.9 %copy-start.1 = (f32[2048,128]{1,0:T(8,128)S(1)}, f32[2048,128]{1,0:T(8,128)}, u32[]{:S(2)}) copy-start(f32[2048,128]{1,0:T(8,128)} %get-tuple-element.45) | copy-start | bytes 3145732
